TPU v7x, 128 devices: a whole 4x4x4 slice. The times are simulated.
128 devices in a mesh: gx: 8 (over y, core), gy: 8 (over x, z_hi), gz: 2 (over z_lo).
Axes of the slice: x: 4, y: 4, z: 4 (z_hi: 2, z_lo: 2; z = z_hi * 2 + z_lo), core: 2. Of those that a mesh axis runs over, the one named last changes fastest.
Arguments:
- positions: float32 [8, 8, 2, 3, 512], P('gx', 'gy', 'gz'), may hold values from 0 to 1
- attributes: bfloat16 [8, 8, 2, 512, 128], P('gx', 'gy', 'gz'), may hold values from -6 to 6
- edge_center: int32 [8, 8, 2, 6144], P('gx', 'gy', 'gz'), may hold values from 0 to 511
- edge_other: int32 [8, 8, 2, 6144], P('gx', 'gy', 'gz'), may hold values from 0 to 2687
- edge_count: int32 [8, 8, 2], P('gx', 'gy', 'gz'), may hold values from 1536 to 6144, as said below
- rim_rows: int32 [8, 8, 2, 8, 128], P('gx', 'gy', 'gz'), may hold values from 0 to 511
- z_rows: int32 [8, 8, 2, 128], P('gx', 'gy', 'gz'), may hold values from 0 to 2559
- w_emb: bfloat16 [128, 256], replicated, may hold values from -0.5 to 0.5
- w_rbf: float32 [8, 256], replicated, may hold values from -2 to 2
- w_chan: bfloat16 [256, 64], replicated, may hold values from -0.375 to 0.375
- w_lat: bfloat16 [256, 256], replicated, may hold values from -0.375 to 0.375
- w_ten: bfloat16 [192, 256], replicated, may hold values from -0.4375 to 0.4375
- w_out: float32 [256], replicated, may hold values from -0.375 to 0.375
Outputs:
- atom_energy: float32 [8, 8, 2, 512], P('gx', 'gy', 'gz')
- forces: float32 [8, 8, 2, 3, 512], P('gx', 'gy', 'gz')
Inputs may be any that keep to these rules, and one draw needn't show every extreme that they name: `edge_count`: a multiple of 128; a device's edge slots below its count are live; some device has 6144.
All inputs are finite; a program needn't handle non-finite values.
Results may differ from a plain program's by a relative error of at most 0.005.
Values may be sent and summed in bfloat16 or wider, within the bound.
A program may use at most 64 MiB of HBM per device.

v0:
```python
import math

import jax
import jax.numpy as jnp
import numpy as np
from jax import lax
from jax.sharding import PartitionSpec as P

rim_cells = [(0, 0), (0, 1), (0, 2), (1, 0), (1, 2), (2, 0), (2, 1), (2, 2)]
cycle_cells = [
    (cycle_row, cycle_column)
    for cycle_row in range(5)
    for cycle_column in range(5)
    if cycle_row in (0, 4) or cycle_column in (0, 4)
]


def padded(cells, sides, width):
    for axis, dim in sides:
        count = lax.axis_size(axis)
        head = lax.slice_in_dim(cells, 0, width, axis=dim)
        tail = lax.slice_in_dim(cells, cells.shape[dim] - width, cells.shape[dim], axis=dim)
        cells = jnp.concatenate(
            [
                lax.ppermute(tail, axis, [(i, (i + 1) % count) for i in range(count)]),
                cells,
                lax.ppermute(head, axis, [((i + 1) % count, i) for i in range(count)]),
            ],
            axis=dim,
        )
    return cells


def swapped(x, axis, distance):
    return lax.ppermute(x, axis, [(i, i ^ 1 << distance) for i in range(lax.axis_size(axis))])


def source_of(position):
    if position == 0:
        return (-1, 2)
    if position == 4:
        return (1, 0)
    return (0, position - 1)


def shift_table():
    listing = []
    for cycle_row, cycle_column in cycle_cells:
        listing.append([source_of(cycle_row)[0], source_of(cycle_column)[0], 0])
    return np.array(listing, np.float32)


def embed_atoms(atom_rows, w_emb):
    return jax.nn.silu(jnp.dot(atom_rows, w_emb, preferred_element_type=jnp.float32)).astype(
        jnp.bfloat16
    )


def split_parts(values):
    upper = lax.optimization_barrier(values.astype(jnp.bfloat16))
    lower = (values - upper.astype(jnp.float32)).astype(jnp.bfloat16)
    return jnp.stack([upper, lower])


def join_parts(parts):
    return parts[0].astype(jnp.float32) + parts[1].astype(jnp.float32)


def harmonics(directions):
    along_x, along_y, along_z = (directions[0], directions[1], directions[2])
    root_three = 3.0**0.5
    return [
        jnp.ones_like(along_x),
        along_x,
        along_y,
        along_z,
        root_three * along_x * along_y,
        root_three * along_y * along_z,
        root_three * along_z * along_x,
        0.5 * root_three * (along_x * along_x - along_y * along_y),
        0.5 * (3.0 * along_z * along_z - 1.0),
    ]


def latent_of(position_table, feature_table, centers, others, w_rbf):
    separation = position_table[:, others] - position_table[:, centers]
    squared = jnp.sum(separation * separation, axis=0)
    distance = jnp.sqrt(squared + 0.25)
    directions = separation / distance[None, :]
    envelope = 1.0 / (1.0 + squared * squared / 16.0)
    radii = 0.5 + 0.4 * jnp.arange(w_rbf.shape[0]).astype(jnp.float32)
    radial = jnp.exp(-jnp.square((distance[None, :] - radii[:, None]) / 0.5)) * envelope[None, :]
    mixed = lax.dot_general(
        radial,
        w_rbf,
        (((0,), (0,)), ((), ())),
        precision=lax.Precision.HIGHEST,
        preferred_element_type=jnp.float32,
    )
    mixed = (
        mixed
        + feature_table[centers].astype(jnp.float32)
        + feature_table[others].astype(jnp.float32)
    )
    return (jax.nn.silu(mixed).astype(jnp.bfloat16), directions, envelope)


def tensor_terms(latent, directions, centers, live_mask, w_chan, atom_count):
    channel = jnp.dot(latent, w_chan, preferred_element_type=jnp.float32) * live_mask[:, None]
    harmonic = harmonics(directions)
    products = jnp.concatenate([channel * term[:, None] for term in harmonic], axis=1)
    return jax.ops.segment_sum(products, centers, num_segments=atom_count)


def energy_terms(latent, directions, envelope, tensor, centers, live_mask, w_lat, w_ten, w_out):
    harmonic = harmonics(directions)
    gathered = tensor[centers]
    width = gathered.shape[1] // 9
    bands = []
    for lower, upper in ((0, 1), (1, 4), (4, 9)):
        band = gathered[:, lower * width : (lower + 1) * width] * harmonic[lower][:, None]
        for index in range(lower + 1, upper):
            band = (
                band + gathered[:, index * width : (index + 1) * width] * harmonic[index][:, None]
            )
        bands.append(band)
    invariant = jnp.concatenate(bands, axis=1).astype(jnp.bfloat16)
    hidden = jax.nn.silu(
        jnp.dot(latent, w_lat, preferred_element_type=jnp.float32)
        + jnp.dot(invariant, w_ten, preferred_element_type=jnp.float32)
    )
    return jnp.sum(hidden * w_out[None, :], axis=1) * envelope * live_mask


def per_device(
    positions,
    attributes,
    edge_center,
    edge_other,
    edge_count,
    rim_rows,
    z_rows,
    w_emb,
    w_rbf,
    w_chan,
    w_lat,
    w_ten,
    w_out,
):
    cycle_shifts = shift_table()
    own_positions = positions[0, 0, 0]
    own_attr = attributes[0, 0, 0]
    centers = edge_center[0, 0, 0]
    others = edge_other[0, 0, 0]
    live_count = edge_count[0, 0, 0]
    rim_index_rows = rim_rows[0, 0, 0]
    slab_rows = z_rows[0, 0, 0]
    atom_count = own_positions.shape[1]
    rim_len = rim_index_rows.shape[1]
    rim_flat = rim_index_rows.reshape(-1)
    own_rows = embed_atoms(own_attr, w_emb)
    row_width = own_rows.shape[1]
    feat_cells = own_rows[rim_flat].reshape(8, rim_len, row_width)
    place_cells = jnp.transpose(
        split_parts(own_positions[:, rim_flat]).reshape(2, 3, 8, rim_len), (2, 0, 1, 3)
    ).reshape(8, -1, row_width)
    packed = jnp.concatenate([feat_cells, place_cells], axis=1)
    empty_cell = jnp.zeros_like(packed[0])
    rim_grid = jnp.stack(
        [
            packed[0],
            packed[1],
            packed[2],
            packed[3],
            empty_cell,
            packed[4],
            packed[5],
            packed[6],
            packed[7],
        ]
    ).reshape((3, 3) + packed.shape[1:])
    halo_grid = padded(rim_grid, (("gx", 0), ("gy", 1)), 1)
    cycle_stack = jnp.stack(
        [halo_grid[cycle_row, cycle_column] for cycle_row, cycle_column in cycle_cells]
    )
    cycle_rows = cycle_stack[:, :rim_len].reshape(-1, row_width)
    cycle_parts = cycle_stack[:, rim_len:].reshape(16, 2, 3, rim_len)
    cycle_positions = (
        join_parts(jnp.transpose(cycle_parts, (1, 2, 0, 3)))
        + jnp.asarray(cycle_shifts.T)[:, :, None]
    )
    inner_rows = jnp.concatenate([own_rows, cycle_rows], axis=0)
    inner_positions = jnp.concatenate([own_positions, cycle_positions.reshape(3, -1)], axis=1)
    slab_len = slab_rows.shape[0]
    slab_parts = split_parts(inner_positions[:, slab_rows]).reshape(-1, row_width)
    slab_got = swapped(jnp.concatenate([inner_rows[slab_rows], slab_parts], axis=0), "gz", 0)
    slab_positions = join_parts(slab_got[slab_len:].reshape(2, 3, slab_len))
    slab_lift = (1 - 2 * lax.axis_index("gz")).astype(jnp.float32)
    slab_positions = slab_positions + slab_lift * jnp.array([0.0, 0.0, 1.0], jnp.float32)[:, None]
    table_rows = jnp.concatenate([inner_rows, slab_got[:slab_len]], axis=0)
    position_table = jnp.concatenate([inner_positions, slab_positions], axis=1)
    edge_total = centers.shape[0]
    block_rows = math.gcd(1024, edge_total)
    block_count = (live_count + block_rows - 1) // block_rows
    tensor_width = w_chan.shape[1] * 9

    def block_slice(block_index):
        first_edge = block_index * block_rows
        block_centers = lax.dynamic_slice_in_dim(centers, first_edge, block_rows)
        block_others = lax.dynamic_slice_in_dim(others, first_edge, block_rows)
        live_mask = (first_edge + jnp.arange(block_rows) < live_count).astype(jnp.float32)
        return (block_centers, block_others, live_mask)

    def first_part(place_values, block_centers, block_others, live_mask):
        latent, directions, envelope = latent_of(
            place_values, table_rows, block_centers, block_others, w_rbf
        )
        return tensor_terms(latent, directions, block_centers, live_mask, w_chan, atom_count)

    def tensor_step(block_index, running):
        block_centers, block_others, live_mask = block_slice(block_index)
        return running + first_part(position_table, block_centers, block_others, live_mask)

    tensor = 0.125 * lax.fori_loop(
        0, block_count, tensor_step, jnp.zeros((atom_count, tensor_width), jnp.float32)
    )

    def energy_step(block_index, totals):
        atom_values, place_grad, tensor_grad = totals
        block_centers, block_others, live_mask = block_slice(block_index)

        def block_energy(place_values, tensor_values):
            latent, directions, envelope = latent_of(
                place_values, table_rows, block_centers, block_others, w_rbf
            )
            return energy_terms(
                latent,
                directions,
                envelope,
                tensor_values,
                block_centers,
                live_mask,
                w_lat,
                w_ten,
                w_out,
            )

        edge_energy, pullback = jax.vjp(block_energy, position_table, tensor)
        grad_place, grad_tensor = pullback(jnp.ones_like(edge_energy))
        atom_values = atom_values + jax.ops.segment_sum(
            edge_energy, block_centers, num_segments=atom_count
        )
        return (atom_values, place_grad + grad_place, tensor_grad + grad_tensor)

    atom_energy, place_grad, tensor_grad = lax.fori_loop(
        0,
        block_count,
        energy_step,
        (
            jnp.zeros((atom_count,), jnp.float32),
            jnp.zeros_like(position_table),
            jnp.zeros_like(tensor),
        ),
    )

    def chain_step(block_index, place_total):
        block_centers, block_others, live_mask = block_slice(block_index)
        unused, pullback = jax.vjp(
            lambda place_values: first_part(place_values, block_centers, block_others, live_mask),
            position_table,
        )
        return place_total + pullback(0.125 * tensor_grad)[0]

    place_grad = lax.fori_loop(0, block_count, chain_step, place_grad)
    inner_len = atom_count + 16 * rim_len
    slab_back = swapped(place_grad[:, inner_len:], "gz", 0)
    inner_grad = place_grad[:, :inner_len].at[:, slab_rows].add(slab_back)
    own_grad = inner_grad[:, :atom_count]
    cycle_grad = jnp.transpose(inner_grad[:, atom_count:].reshape(3, 16, rim_len), (1, 0, 2))
    halo_back = jnp.zeros((5, 5, 3, rim_len), jnp.float32)
    for cycle_index, (cycle_row, cycle_column) in enumerate(cycle_cells):
        halo_back = halo_back.at[cycle_row, cycle_column].set(cycle_grad[cycle_index])
    rim_back = jnp.zeros((3, 3, 3, rim_len), jnp.float32)
    column_got = padded(jnp.stack([halo_back[:, 0], halo_back[:, 4]]), (("gy", 0),), 1)
    rim_back = rim_back.at[:, 0].add(column_got[0, 1:4]).at[:, 2].add(column_got[3, 1:4])
    halo_back = halo_back.at[0, 1].add(column_got[0, 0]).at[4, 1].add(column_got[0, 4])
    halo_back = halo_back.at[0, 3].add(column_got[3, 0]).at[4, 3].add(column_got[3, 4])
    row_got = padded(jnp.stack([halo_back[0, 1:4], halo_back[4, 1:4]]), (("gx", 0),), 1)
    rim_back = rim_back.at[0].add(row_got[0]).at[2].add(row_got[3])
    rim_stack = jnp.stack([rim_back[cell_row, cell_column] for cell_row, cell_column in rim_cells])
    own_grad = own_grad.at[:, rim_flat].add(jnp.transpose(rim_stack, (1, 0, 2)).reshape(3, -1))
    return (atom_energy[None, None, None], (-own_grad)[None, None, None])


def solution(mesh):
    return jax.shard_map(
        per_device,
        mesh=mesh,
        in_specs=(
            P("gx", "gy", "gz", None, None),
            P("gx", "gy", "gz", None, None),
            P("gx", "gy", "gz", None),
            P("gx", "gy", "gz", None),
            P("gx", "gy", "gz"),
            P("gx", "gy", "gz", None, None),
            P("gx", "gy", "gz", None),
            P(),
            P(),
            P(),
            P(),
            P(),
            P(),
        ),
        out_specs=(P("gx", "gy", "gz", None), P("gx", "gy", "gz", None, None)),
        check_vma=False,
    )
```

profile of v0, /device:TPU:1, one launch (start us, length us, event | category | flops | bytes accessed | tf_op | source)
XLA Modules:
  0.0 1308.1 jit_solution(1081782127686385945)
XLA Ops:
  24.1 10.6 collective-permute-done.2
  54.2 130.6 %while.64 = (s32[]{:T(128)}, f32[512,576]{1,0:T(8,128)S(1)}, s32[]{:T(128)}, s32[6144]{0:T(1024)}, s32[6144]{0:T(1024)}, /*index=5*/f32[3,2688]{0,1:T(8,128)}, f...) while((s32[]{:T(128)}, f32[512,576]{1,0:T(8,128)S(1)}, ...), condition=%wide.region_3.4_spmd, body=%wide.region_0.3_spmd.sunk | while | flops 62342172 | bytes 25223488 | solution.py:224
  89.4 8.4 scatter_fusion
  132.9 8.4 scatter_fusion
  176.4 8.4 scatter_fusion
  187.4 306.9 %while.65 = (s32[]{:T(128)}, f32[512]{0:T(512)S(1)}, f32[3,2688]{0,1:T(8,128)}, f32[512,576]{1,0:T(8,128)S(1)}, s32[]{:T(128)}, /*index=5*/s32[6144]{0:T(1024)},...) while((s32[]{:T(128)}, f32[512]{0:T(512)S(1)}, ...), condition=%wide.region_21.22_spmd, body=%wide.region_4.21_spmd.sunk | while | flops 542212096 | bytes 73343152 | solution.py:255
  200.1 6.8 gather_fusion.6
  249.7 7.6 scatter_fusion.1
  260.0 13.1 %scatter_fusion.2 = f32[3,2688]{0,1:T(8,128)} fusion(f32[3,2688]{0,1:T(8,128)} %get-tuple-element.1610, s32[2048]{0:T(1024)} %bitcast.399, f32[2048,3]{1,0:T(8,128)} %copy.307), kind=kCustom, calls=%fused_computation.20.clone.1 | custom fusion | flops 6144 | bytes 81920 | tf_op jit(solution)/shard_map/while/body/transpose(jvp())/add_any | solution.py:86
  278.2 8.4 scatter_fusion.3
  299.0 6.8 gather_fusion.6
  348.6 7.6 scatter_fusion.1
  358.9 13.1 %scatter_fusion.2 = f32[3,2688]{0,1:T(8,128)} fusion(f32[3,2688]{0,1:T(8,128)} %get-tuple-element.1610, s32[2048]{0:T(1024)} %bitcast.399, f32[2048,3]{1,0:T(8,128)} %copy.307), kind=kCustom, calls=%fused_computation.20.clone.1 | custom fusion | flops 6144 | bytes 81920 | tf_op jit(solution)/shard_map/while/body/transpose(jvp())/add_any | solution.py:86
  377.1 8.4 scatter_fusion.3
  397.9 6.8 gather_fusion.6
  447.5 7.6 scatter_fusion.1
  457.9 13.1 %scatter_fusion.2 = f32[3,2688]{0,1:T(8,128)} fusion(f32[3,2688]{0,1:T(8,128)} %get-tuple-element.1610, s32[2048]{0:T(1024)} %bitcast.399, f32[2048,3]{1,0:T(8,128)} %copy.307), kind=kCustom, calls=%fused_computation.20.clone.1 | custom fusion | flops 6144 | bytes 81920 | tf_op jit(solution)/shard_map/while/body/transpose(jvp())/add_any | solution.py:86
  476.0 8.4 scatter_fusion.3
  494.8 172.4 %while.66 = (s32[]{:T(128)}, f32[3,2688]{0,1:T(8,128)}, s32[]{:T(128)}, s32[6144]{0:T(1024)}, s32[6144]{0:T(1024)}, /*index=5*/f32[3,2688]{0,1:T(8,128)}, f32[8,...) while((s32[]{:T(128)}, f32[3,2688]{0,1:T(8,128)}, ...), condition=%wide.region_36.37_spmd, body=%wide.region_22.36_spmd.sunk | while | flops 126082080 | bytes 29296976 | solution.py:274
  539.2 13.1 %scatter_fusion.4 = f32[3,2688]{0,1:T(8,128)} fusion(f32[3,2688]{0,1:T(8,128)} %get-tuple-element.1662, s32[2048]{0:T(1024)S(1)} %bitcast.398, f32[2048,3]{1,0:T(8,128)} %copy.312), kind=kCustom, calls=%fused_computation.22.clone.1 | custom fusion | flops 6144 | bytes 81920 | tf_op jit(solution)/shard_map/while/body/transpose(jvp())/add_any | solution.py:86
  596.7 13.1 %scatter_fusion.4 = f32[3,2688]{0,1:T(8,128)} fusion(f32[3,2688]{0,1:T(8,128)} %get-tuple-element.1662, s32[2048]{0:T(1024)S(1)} %bitcast.398, f32[2048,3]{1,0:T(8,128)} %copy.312), kind=kCustom, calls=%fused_computation.22.clone.1 | custom fusion | flops 6144 | bytes 81920 | tf_op jit(solution)/shard_map/while/body/transpose(jvp())/add_any | solution.py:86
  654.1 13.1 %scatter_fusion.4 = f32[3,2688]{0,1:T(8,128)} fusion(f32[3,2688]{0,1:T(8,128)} %get-tuple-element.1662, s32[2048]{0:T(1024)S(1)} %bitcast.398, f32[2048,3]{1,0:T(8,128)} %copy.312), kind=kCustom, calls=%fused_computation.22.clone.1 | custom fusion | flops 6144 | bytes 81920 | tf_op jit(solution)/shard_map/while/body/transpose(jvp())/add_any | solution.py:86
  685.1 201.0 %collective-permute-start.7 = (f32[1,5,3,128]{3,1,2,0:T(8,128)S(1)}, f32[1,5,3,128]{3,1,2,0:T(8,128)S(1)}, u32[]{:S(2)}, u32[]{:S(2)}) collective-permute-start(f32[1,5,3,128]{3,1,2,0:T(8,128)S(1)} %copy.256), channel_id=1, source_target_pairs={{2,0},{4,2},{6,4},{8,6},{10,8},{12,10},{14,12},{0,14},{3,1},{5,3},... | collective-permute-start | bytes 23048 | tf_op jit(solution)/shard_map/ppermute | solution.py:27
  889.7 398.1 %collective-permute-done.7 = f32[1,5,3,128]{3,1,2,0:T(8,128)S(1)} collective-permute-done((f32[1,5,3,128]{3,1,2,0:T(8,128)S(1)}, f32[1,5,3,128]{3,1,2,0:T(8,128)S(1)}, u32[]{:S(2)}, u32[]{:S(2)}) %collective-permute-start.7) | collective-permute-done | bytes 7712 | tf_op jit(solution)/shard_map/ppermute | solution.py:27
  (637 shorter events, 511.9 us)
Async XLA Ops:
  11.3 6.2 collective-permute-start.1
  12.8 4.8 collective-permute-start
  17.6 17.1 %collective-permute-start.2 = (bf16[5,1,131,256]{3,2,1,0:T(8,128)(2,1)S(1)}, bf16[5,1,131,256]{3,2,1,0:T(8,128)(2,1)S(1)}, u32[]{:S(2)}, u32[]{:S(2)}) collective-permute-start(bf16[5,1,131,256]{3,2,1,0:T(8,128)(2,1)S(1)} %get-tuple-element.1064), channel_id=1, source_target_pairs={{0,2},{2,4},{4,6},{6,8},{8,10},{10,12},{12,14},{14,0},{1,3},{3,5},... | collective-permute-start | bytes 1006088 | tf_op jit(solution)/shard_map/ppermute | solution.py:25
  21.9 16.9 %collective-permute-start.3 = (bf16[5,1,131,256]{3,2,1,0:T(8,128)(2,1)S(1)}, bf16[5,1,131,256]{3,2,1,0:T(8,128)(2,1)S(1)}, u32[]{:S(2)}, u32[]{:S(2)}) collective-permute-start(bf16[5,1,131,256]{3,2,1,0:T(8,128)(2,1)S(1)} %get-tuple-element.1063), channel_id=1, source_target_pairs={{2,0},{4,2},{6,4},{8,6},{10,8},{12,10},{14,12},{0,14},{3,1},{5,3},... | collective-permute-start | bytes 1006088 | tf_op jit(solution)/shard_map/ppermute | solution.py:27
  48.5 3.2 collective-permute-start.4
  193.9 13.0 copy-start.19
  198.3 8.6 copy-start.17
  249.7 7.6 copy-start.24
  249.7 7.6 copy-start.26
  257.3 15.8 %copy-start.12 = (f32[1024,192]{0,1:T(8,128)S(1)}, f32[1024,192]{0,1:T(8,128)}, u32[]{:S(2)}) copy-start(f32[1024,192]{0,1:T(8,128)} %copy-done.11) | copy-start | bytes 2359300 | tf_op jit(solution)/shard_map/while
  292.8 13.0 copy-start.19
  297.2 8.6 copy-start.17
  348.6 7.6 copy-start.24
  356.2 15.8 %copy-start.12 = (f32[1024,192]{0,1:T(8,128)S(1)}, f32[1024,192]{0,1:T(8,128)}, u32[]{:S(2)}) copy-start(f32[1024,192]{0,1:T(8,128)} %copy-done.11) | copy-start | bytes 2359300 | tf_op jit(solution)/shard_map/while
  391.7 13.0 copy-start.19
  396.1 8.6 copy-start.17
  455.1 15.8 %copy-start.12 = (f32[1024,192]{0,1:T(8,128)S(1)}, f32[1024,192]{0,1:T(8,128)}, u32[]{:S(2)}) copy-start(f32[1024,192]{0,1:T(8,128)} %copy-done.11) | copy-start | bytes 2359300 | tf_op jit(solution)/shard_map/while
  668.1 3.1 collective-permute-start.5
  673.1 627.9 %copy-start.29 = (s32[1024,1]{0,1:T(1,128)S(1)}, s32[1024,1]{0,1:T(1,128)}, u32[]{:S(2)}) copy-start(s32[1024,1]{0,1:T(1,128)} %copy-done.28) | copy-start | bytes 12292
  684.3 623.6 %copy-start.1 = (bf16[1,1,1,512,128]{4,3,2,1,0:T(8,128)(2,1)S(1)}, bf16[1,1,1,512,128]{4,3,2,1,0:T(8,128)(2,1)}, u32[]{:S(2)}) copy-start(bf16[1,1,1,512,128]{4,3,2,1,0:T(8,128)(2,1)} %param.70) | copy-start | bytes 393220
  685.0 202.0 %collective-permute-start.6 = (f32[1,5,3,128]{3,1,2,0:T(8,128)S(1)}, f32[1,5,3,128]{3,1,2,0:T(8,128)S(1)}, u32[]{:S(2)}, u32[]{:S(2)}) collective-permute-start(f32[1,5,3,128]{3,1,2,0:T(8,128)S(1)} %copy.255), channel_id=1, source_target_pairs={{0,2},{2,4},{4,6},{6,8},{8,10},{10,12},{12,14},{14,0},{1,3},{3,5},... | collective-permute-start | bytes 23048 | tf_op jit(solution)/shard_map/ppermute | solution.py:25
  685.1 602.8 %collective-permute-start.7 = (f32[1,5,3,128]{3,1,2,0:T(8,128)S(1)}, f32[1,5,3,128]{3,1,2,0:T(8,128)S(1)}, u32[]{:S(2)}, u32[]{:S(2)}) collective-permute-start(f32[1,5,3,128]{3,1,2,0:T(8,128)S(1)} %copy.256), channel_id=1, source_target_pairs={{2,0},{4,2},{6,4},{8,6},{10,8},{12,10},{14,12},{0,14},{3,1},{5,3},... | collective-permute-start | bytes 23048 | tf_op jit(solution)/shard_map/ppermute | solution.py:27
  1291.2 3.0 collective-permute-start.9
  1291.3 9.4 collective-permute-start.8
  (83 other events, 211.8 us)
where the time goes:
time: 1330 us; the launch traced here: 1310 us
  waiting for transfers between devices  425 us (32%)
  local copies, waits for them, and re-layouts  340 us (26%)
  other arithmetic  255 us (19%)
  starting transfers between devices  212 us (16%)
  matrix products  62 us (5%)
    ppermute x4, waiting for transfers between devices, padded(): lax.ppermute(head, axis, [((i + 1) % count, i) for i in range(count)])  404 us
    ppermute x4, starting transfers between devices, padded(): lax.ppermute(head, axis, [((i + 1) % count, i) for i in range(count)])  205 us
    gather x30, local copies, waits for them, and re-layouts, latent_of(): separation = position_table[:, others] - position_table[:, centers]  80.4 us
    add_any x6, other arithmetic, latent_of(): separation = position_table[:, others] - position_table[:, centers]  78.6 us
    gather x9, local copies, waits for them, and re-layouts, latent_of(): feature_table[centers].astype(jnp.float32)  45.5 us
    gather x9, local copies, waits for them, and re-layouts, latent_of(): feature_table[others].astype(jnp.float32)  41.4 us
    while x201, local copies, waits for them, and re-layouts  40 us
    dot_general x15, matrix products, latent_of(): lax.dot_general(radial, w_rbf, (((0,), (0,)), ((), ())), precision=lax.Pr...  32.6 us
  transfers between devices with their start and end apart: 10, of which 9 were waited for; matrix products, arithmetic and copies ran while one was open for 1% of the time, Pallas kernels for 0%

commit v1 on v0

v1 whole, which is shorter than its diff:
```python
import functools

import jax
import jax.numpy as jnp
from jax import lax
from jax.experimental import pallas as pl
from jax.experimental.pallas import tpu as pltpu
from jax.sharding import PartitionSpec as P

F32, BF16, I32 = jnp.float32, jnp.bfloat16, jnp.int32
ROOT3 = 3.0 ** 0.5
BANDS = (0, 1, 1, 1, 2, 2, 2, 2, 2)


def nt(a, b):
    return lax.dot_general(a, b, (((1,), (1,)), ((), ())), preferred_element_type=F32)


def nn(a, b):
    return jnp.dot(a, b, preferred_element_type=F32)


def turned(w, unit):
    return lax.dot_general(w, unit, (((0,), (0,)), ((), ())), preferred_element_type=F32).astype(BF16)


def sigmoid(x):
    return 0.5 * jnp.tanh(0.5 * x) + 0.5


def eye(n):
    rows = lax.broadcasted_iota(I32, (n, n), 0)
    cols = lax.broadcasted_iota(I32, (n, n), 1)
    return jnp.where(rows == cols, 1.0, 0.0).astype(BF16)


def three_parts(v):
    upper = v.astype(BF16).astype(F32)
    rest = v - upper
    middle = rest.astype(BF16).astype(F32)
    return upper, middle, rest - middle


def hits(rows, index_row, offset, width):
    ids = lax.broadcasted_iota(I32, (rows, width), 0) + offset
    return jnp.where(ids == index_row, 1.0, 0.0).astype(BF16)


def edge_kernel(
    attr_ref, pos_ref, center_ref, other_ref, w_emb_ref, w_rbf_ref, w_chan_ref, w_lat_ref, w_ten_ref,
    w_out_ref, energy_ref, grad_ref,
    tab, one_c, lat_s, dsilu_s, dlat_s, chan_s, geo_s, dh_s, tens, tens_b, wrt, wct, wlt, wtt, wback, wr2, wout_c,
    *, nb, eb, atoms, tbl,
):
    feat = w_emb_ref.shape[1]
    adim = w_emb_ref.shape[0]
    ch = w_chan_ref.shape[1]
    nbas = w_rbf_ref.shape[0]
    big_eye = eye(feat)
    emb_t = turned(w_emb_ref[...], eye(adim))
    wct[...] = turned(w_chan_ref[...], big_eye)
    wlt[...] = turned(w_lat_ref[...], big_eye)
    wtt[...] = turned(w_ten_ref[...], eye(3 * ch))
    wback[0:feat, :] = w_lat_ref[...]
    wback[feat:, :] = w_ten_ref[...]
    rb = w_rbf_ref[...]
    rb_hi = rb.astype(BF16).astype(F32)
    rb_lo = rb - rb_hi
    wr2[...] = jnp.concatenate([rb_hi, rb_lo], axis=0).astype(BF16)
    wrt[...] = nt(big_eye, jnp.concatenate([rb_hi, rb_hi, rb_lo, rb_lo], axis=0).astype(BF16)).astype(BF16)
    wo = w_out_ref[...]
    wout_c[...] = jnp.sum(jnp.where(
        lax.broadcasted_iota(I32, (feat, feat), 0) == lax.broadcasted_iota(I32, (feat, feat), 1),
        jnp.broadcast_to(wo, (feat, feat)), 0.0), axis=1, keepdims=True)

    emb = nn(emb_t, attr_ref[...])
    emb = (emb * sigmoid(emb)).astype(BF16)
    tab[0:feat, 0:tbl] = emb
    tab[0:feat, tbl:] = emb[:, 0:atoms]
    p3 = three_parts(pos_ref[...][0:3])
    rows = jnp.concatenate(list(p3) + [jnp.zeros((7, tbl), F32)], axis=0)
    tab[feat:, 0:tbl] = rows.astype(BF16)
    tab[feat:, tbl:] = (-rows[:, 0:atoms]).astype(BF16)

    tens[...] = jnp.zeros_like(tens)

    def geometry(sep):
        sq = jnp.sum(sep * sep, axis=0, keepdims=True)
        inv = lax.rsqrt(sq + 0.25)
        dist = (sq + 0.25) * inv
        env = 1.0 / (1.0 + sq * sq * (1.0 / 16.0))
        radii = 0.5 + 0.4 * lax.broadcasted_iota(I32, (nbas, 1), 0).astype(F32)
        t = (dist - radii) * 2.0
        gauss = jnp.exp(-(t * t))
        return sq, inv, dist, env, t, gauss

    def phase1(b, _):
        c_row = center_ref[b]
        o_row = other_ref[b]
        a_o = hits(tbl, o_row, 0, eb)
        a_c = hits(atoms, c_row, 0, eb)
        one_c[b] = a_c
        m1 = nn(tab[:, 0:tbl], a_o) + nn(tab[:, tbl:], a_c)
        sep = m1[feat:feat + 3] + m1[feat + 3:feat + 6] + m1[feat + 6:feat + 9]
        sq, inv, dist, env, t, gauss = geometry(sep)
        radial = gauss * env
        r_hi = radial.astype(BF16).astype(F32)
        r_lo = radial - r_hi
        parts = jnp.concatenate([r_hi, r_lo, r_hi, r_lo], axis=0).astype(BF16)
        mixed = m1[0:feat] + nn(wrt[...], parts)
        s = sigmoid(mixed)
        latent = (mixed * s).astype(BF16)
        lat_s[b] = latent
        dsilu_s[b] = (s * (1.0 + mixed * (1.0 - s))).astype(BF16)
        chan = nn(wct[...], latent)
        chan_s[b] = chan
        dirs = sep * inv
        x, y, z = dirs[0:1], dirs[1:2], dirs[2:3]
        harm = jnp.concatenate([
            jnp.ones_like(x), x, y, z, ROOT3 * x * y, ROOT3 * y * z, ROOT3 * z * x,
            0.5 * ROOT3 * (x * x - y * y), 0.5 * (3.0 * z * z - 1.0),
            sep, env, jnp.zeros((3, eb), F32)], axis=0)
        geo_s[b] = harm
        prod = jnp.concatenate([chan] + [chan * harm[m:m + 1] for m in range(1, 9)], axis=0).astype(BF16)
        tens[0:9 * ch] += nt(prod, a_c)
        return 0

    lax.fori_loop(0, nb, phase1, 0)
    tens_b[...] = (0.125 * tens[0:9 * ch]).astype(BF16)
    tens[...] = jnp.zeros_like(tens)

    def phase2(b, _):
        a_c = one_c[b]
        harm = geo_s[b]
        env = harm[12:13]
        latent = lat_s[b]
        gath = nn(tens_b[...], a_c)
        g = [gath[m * ch:(m + 1) * ch] for m in range(9)]
        h = [harm[m:m + 1] for m in range(9)]
        inv0 = g[0]
        inv1 = g[1] * h[1] + g[2] * h[2] + g[3] * h[3]
        inv2 = g[4] * h[4] + g[5] * h[5] + g[6] * h[6] + g[7] * h[7] + g[8] * h[8]
        invb = jnp.concatenate([inv0, inv1, inv2], axis=0).astype(BF16)
        pre = nn(wlt[...], latent) + nn(wtt[...], invb)
        s = sigmoid(pre)
        wo = wout_c[...]
        e = jnp.sum(pre * s * wo, axis=0, keepdims=True)
        dpre = (s * (1.0 + pre * (1.0 - s))) * wo * env
        back = nn(wback[...], dpre.astype(BF16))
        dlat_s[b] = back[0:feat]
        dinv = [back[feat + l * ch:feat + (l + 1) * ch] for l in range(3)]
        dh = [jnp.sum(dinv[BANDS[m]] * g[m], axis=0, keepdims=True) for m in range(1, 9)]
        en = e * env
        dh_s[b] = jnp.concatenate([e] + dh + [jnp.zeros((7, eb), F32)], axis=0)
        en_hi = en.astype(BF16).astype(F32)
        prod = jnp.concatenate(
            [dinv[0]] + [dinv[BANDS[m]] * h[m] for m in range(1, 9)] + [en_hi, en - en_hi, jnp.zeros((14, eb), F32)],
            axis=0).astype(BF16)
        tens[...] += nt(prod, a_c)
        return 0

    lax.fori_loop(0, nb, phase2, 0)
    energy_ref[...] = tens[9 * ch:9 * ch + 1] + tens[9 * ch + 1:9 * ch + 2]
    tens_b[...] = (0.125 * tens[0:9 * ch]).astype(BF16)
    grad_ref[...] = jnp.zeros_like(grad_ref)
    nqo, nqc = tbl // 128, atoms // 128

    def phase3(b, _):
        a_c = one_c[b]
        harm = geo_s[b]
        gd = nn(tens_b[...], a_c)
        g = [gd[m * ch:(m + 1) * ch] for m in range(9)]
        h = [harm[m:m + 1] for m in range(9)]
        chan = chan_s[b]
        dchan = g[0]
        for m in range(1, 9):
            dchan = dchan + g[m] * h[m]
        old = dh_s[b]
        k = [None] + [old[m:m + 1] + jnp.sum(chan * g[m], axis=0, keepdims=True) for m in range(1, 9)]
        dlat = dlat_s[b] + nn(w_chan_ref[...], dchan.astype(BF16))
        dmixed = (dlat * dsilu_s[b].astype(F32)).astype(BF16)
        d16 = nn(wr2[...], dmixed)
        drad = d16[0:nbas] + d16[nbas:]
        sep = harm[9:12]
        sq, inv, dist, env, t, gauss = geometry(sep)
        dg = drad * gauss
        d_dist = jnp.sum(dg * t, axis=0, keepdims=True) * (-4.0 * env)
        d_env = jnp.sum(dg, axis=0, keepdims=True) + old[0:1]
        x, y, z = h[1], h[2], h[3]
        dx = k[1] + ROOT3 * (y * k[4] + z * k[6] + x * k[7])
        dy = k[2] + ROOT3 * (x * k[4] + z * k[5] - y * k[7])
        dz = k[3] + ROOT3 * (y * k[5] + x * k[6]) + 3.0 * z * k[8]
        d_dist = d_dist - (dx * x + dy * y + dz * z) * inv
        d_sq = d_dist * (0.5 * inv) - d_env * env * env * sq * 0.125
        dsep = jnp.concatenate([dx, dy, dz], axis=0) * inv + sep * (2.0 * d_sq)
        hi = dsep.astype(BF16).astype(F32)
        d8 = jnp.concatenate([hi, dsep - hi, jnp.zeros((2, eb), F32)], axis=0)
        o_row, c_row = other_ref[b], center_ref[b]
        oq, cq = o_row >> 7, c_row >> 7
        lhs = jnp.concatenate(
            [jnp.where(oq == q, d8, 0.0) for q in range(nqo)] + [jnp.where(cq == q, d8, 0.0) for q in range(nqc)],
            axis=0).astype(BF16)
        rhs = jnp.concatenate([hits(128, o_row & 127, 0, eb), hits(128, c_row & 127, 0, eb)], axis=0)
        grad_ref[...] += nt(lhs, rhs)
        return 0

    lax.fori_loop(0, nb, phase3, 0)


def edge_call(attr_t, pos8, centers, others, w_emb, w_rbf, w_chan, w_lat, w_ten, w_out, eb=512):
    feat, ch, tbl, atoms = w_emb.shape[1], w_chan.shape[1], attr_t.shape[1], 512
    edges = centers.shape[0]
    nb = edges // eb
    V = pltpu.VMEM
    spec = pl.BlockSpec(memory_space=pltpu.VMEM)
    return pl.pallas_call(
        functools.partial(edge_kernel, nb=nb, eb=eb, atoms=atoms, tbl=tbl),
        out_shape=(jax.ShapeDtypeStruct((1, atoms), F32), jax.ShapeDtypeStruct(((tbl + atoms) // 128 * 8, 256), F32)),
        in_specs=[spec] * 10, out_specs=(spec, spec),
        scratch_shapes=[
            V((feat + 16, tbl + atoms), BF16), V((nb, atoms, eb), BF16), V((nb, feat, eb), BF16), V((nb, feat, eb), BF16),
            V((nb, feat, eb), F32), V((nb, ch, eb), F32), V((nb, 16, eb), F32), V((nb, 16, eb), F32),
            V((9 * ch + 16, atoms), F32), V((9 * ch, atoms), BF16),
            V((feat, 32), BF16), V((ch, feat), BF16), V((feat, feat), BF16), V((feat, 3 * ch), BF16),
            V((feat + 3 * ch, feat), BF16), V((16, feat), BF16), V((feat, 1), F32)],
        compiler_params=pltpu.CompilerParams(vmem_limit_bytes=60 << 20),
        name="edges",
    )(attr_t, pos8, centers.reshape(nb, 1, eb), others.reshape(nb, 1, eb), w_emb, w_rbf, w_chan, w_lat, w_ten, w_out.reshape(1, -1))


MESH = pl.DeviceIdType.MESH
RIM_CELLS = [(0, 0), (0, 1), (0, 2), (1, 0), (1, 2), (2, 0), (2, 1), (2, 2)]


def source_of(position):
    if position == 0:
        return (-1, 2)
    if position == 4:
        return (1, 0)
    return (0, position - 1)


LINKS = []
for row in range(5):
    for column in range(5):
        if row in (0, 4) or column in (0, 4):
            sx, ra = source_of(row)
            sy, rb = source_of(column)
            LINKS.append((len(LINKS), RIM_CELLS.index((ra, rb)), sx, sy))
SEND_ORDER = sorted(LINKS, key=lambda link: -(3 * abs(link[3]) + abs(link[2])))


def places():
    i, j, k = (lax.axis_index(name) for name in ("gx", "gy", "gz"))
    nx, ny = lax.axis_size("gx"), lax.axis_size("gy")

    def at(sx, sy):
        return (lax.rem(i + (sx + nx), nx), lax.rem(j + (sy + ny), ny), k)

    return at, (i, j, 1 - k), k


def greet(at, partner):
    barrier = pltpu.get_barrier_semaphore()
    for sx in (-1, 0, 1):
        for sy in (-1, 0, 1):
            if sx or sy:
                pl.semaphore_signal(barrier, inc=1, device_id=at(sx, sy), device_id_type=MESH)
    pl.semaphore_signal(barrier, inc=1, device_id=partner, device_id_type=MESH)
    pl.semaphore_wait(barrier, 9)


def two_parts(v):
    upper = v.astype(BF16).astype(F32)
    return upper, v - upper


def table_kernel(
    attr_ref, pos_ref, rim_ref, z_ref, table_ref, place_ref,
    cells, got, zcell, zgot, inner, send_sem, recv_sem, zsend, zrecv,
):
    at, partner, k = places()
    adim, atoms = attr_ref.shape[1], attr_ref.shape[0]
    rim_len = rim_ref.shape[1]
    attr_t = nt(eye(adim), attr_ref[...])
    pos = pos_ref[...]
    hi, lo = two_parts(pos)
    pad = jnp.zeros((10, atoms), F32)
    own = jnp.concatenate([attr_t, hi, lo, pad], axis=0).astype(BF16)
    inner[:, 0:atoms] = own
    table_ref[:, 0:atoms] = own[0:adim]
    place_ref[:, 0:atoms] = jnp.concatenate([pos, jnp.zeros((5, atoms), F32)], axis=0)
    for c in range(8):
        cells[c] = nn(own, hits(atoms, rim_ref[c:c + 1, :], 0, rim_len)).astype(BF16)
    greet(at, partner)

    def link_copy(slot, cell, sx, sy):
        return pltpu.make_async_remote_copy(
            src_ref=cells.at[cell], dst_ref=got.at[slot], send_sem=send_sem.at[slot], recv_sem=recv_sem.at[slot],
            device_id=at(-sx, -sy), device_id_type=MESH)

    for link in SEND_ORDER:
        link_copy(*link).start()
    for slot, cell, sx, sy in SEND_ORDER[::-1]:
        link_copy(slot, cell, sx, sy).wait_recv()
        block = got[slot]
        first = atoms + slot * rim_len
        table_ref[:, first:first + rim_len] = block[0:adim]
        tail = block[adim:].astype(F32)
        rows = lax.broadcasted_iota(I32, (3, rim_len), 0)
        shift = jnp.where(rows == 0, float(sx), jnp.where(rows == 1, float(sy), 0.0))
        moved = tail[0:3] + tail[3:6] + shift
        place_ref[:, first:first + rim_len] = jnp.concatenate([moved, jnp.zeros((5, rim_len), F32)], axis=0)
        hi, lo = two_parts(moved)
        inner[0:adim, first:first + rim_len] = block[0:adim]
        inner[adim:, first:first + rim_len] = jnp.concatenate([hi, lo, pad[:, 0:rim_len]], axis=0).astype(BF16)
    inner_len = inner.shape[1]
    zlen = z_ref.shape[1]
    zcell[...] = nn(inner[...], hits(inner_len, z_ref[...], 0, zlen)).astype(BF16)
    zcopy = pltpu.make_async_remote_copy(
        src_ref=zcell, dst_ref=zgot, send_sem=zsend, recv_sem=zrecv, device_id=partner, device_id_type=MESH)
    zcopy.start()
    zcopy.wait_recv()
    block = zgot[...]
    table_ref[:, inner_len:] = block[0:adim]
    tail = block[adim:].astype(F32)
    lift = (1 - 2 * k).astype(F32)
    rows = lax.broadcasted_iota(I32, (3, zlen), 0)
    moved = tail[0:3] + tail[3:6] + jnp.where(rows == 2, lift, 0.0)
    place_ref[:, inner_len:] = jnp.concatenate([moved, jnp.zeros((5, zlen), F32)], axis=0)
    for link in LINKS:
        link_copy(*link).wait_send()
    zcopy.wait_send()


def table_call(attr, pos, rim, z):
    atoms, adim = attr.shape
    rim_len, zlen = rim.shape[1], z.shape[1]
    inner_len = atoms + 16 * rim_len
    V, D = pltpu.VMEM, pltpu.SemaphoreType.DMA
    spec = pl.BlockSpec(memory_space=pltpu.VMEM)
    return pl.pallas_call(
        table_kernel,
        out_shape=(jax.ShapeDtypeStruct((adim, inner_len + zlen), BF16), jax.ShapeDtypeStruct((8, inner_len + zlen), F32)),
        in_specs=[spec] * 4, out_specs=(spec, spec),
        scratch_shapes=[
            V((8, adim + 16, rim_len), BF16), V((16, adim + 16, rim_len), BF16), V((adim + 16, zlen), BF16),
            V((adim + 16, zlen), BF16), V((adim + 16, inner_len), BF16), D((16,)), D((16,)), D, D],
        compiler_params=pltpu.CompilerParams(collective_id=0, has_side_effects=True, vmem_limit_bytes=32 << 20),
        name="table",
    )(attr, pos, rim, z)


def force_kernel(
    grad_ref, rim_ref, z_ref, force_ref,
    slab, slab_got, cells, got, send_sem, recv_sem, zsend, zrecv,
):
    at, partner, k = places()
    atoms = force_ref.shape[1]
    rim_len, zlen = rim_ref.shape[1], z_ref.shape[1]
    nqc = atoms // 128
    nqo = grad_ref.shape[0] // 8 - nqc

    def summed(block):
        return block[0:3] + block[3:6]

    slab[...] = grad_ref[(nqo - 1) * 8:nqo * 8, 0:128]
    greet(at, partner)
    zcopy = pltpu.make_async_remote_copy(
        src_ref=slab, dst_ref=slab_got, send_sem=zsend, recv_sem=zrecv, device_id=partner, device_id_type=MESH)
    zcopy.start()
    own = jnp.concatenate(
        [summed(grad_ref[q * 8:(q + 1) * 8, 0:128]) - summed(grad_ref[(nqo + q) * 8:(nqo + q + 1) * 8, 128:256])
         for q in range(nqc)], axis=1)
    zcopy.wait_recv()
    back = jnp.concatenate(list(three_parts(summed(slab_got[...]))) + [jnp.zeros((7, zlen), F32)], axis=0).astype(BF16)
    z_row = z_ref[...]
    own_back = nt(back, hits(atoms, z_row, 0, zlen))
    own = own + own_back[0:3] + own_back[3:6] + own_back[6:9]
    spread = nt(back, hits(16 * rim_len, z_row, atoms, zlen))
    spread = spread[0:3] + spread[3:6] + spread[6:9]
    for slot in range(16):
        q = nqc + slot
        cells[slot, 0:3] = summed(grad_ref[q * 8:(q + 1) * 8, 0:128]) + spread[:, slot * rim_len:(slot + 1) * rim_len]
        cells[slot, 3:8] = jnp.zeros((5, rim_len), F32)

    def link_copy(slot, cell, sx, sy):
        return pltpu.make_async_remote_copy(
            src_ref=cells.at[slot], dst_ref=got.at[slot], send_sem=send_sem.at[slot], recv_sem=recv_sem.at[slot],
            device_id=at(sx, sy), device_id_type=MESH)

    for link in SEND_ORDER:
        link_copy(*link).start()
    for link in SEND_ORDER[::-1]:
        link_copy(*link).wait_recv()
    rim_back = []
    for cell in range(8):
        rim_back.append(sum(got[slot][0:3] for slot, c, sx, sy in LINKS if c == cell))
    total = jnp.concatenate(rim_back, axis=1)
    parts = jnp.concatenate(list(three_parts(total)) + [jnp.zeros((7, 8 * rim_len), F32)], axis=0).astype(BF16)
    for cell in range(8):
        add = nt(parts[:, cell * rim_len:(cell + 1) * rim_len], hits(atoms, rim_ref[cell:cell + 1, :], 0, rim_len))
        own = own + add[0:3] + add[3:6] + add[6:9]
    force_ref[...] = -own
    for link in LINKS:
        link_copy(*link).wait_send()
    zcopy.wait_send()


def force_call(grad, rim, z, atoms):
    rim_len, zlen = rim.shape[1], z.shape[1]
    V, D = pltpu.VMEM, pltpu.SemaphoreType.DMA
    spec = pl.BlockSpec(memory_space=pltpu.VMEM)
    return pl.pallas_call(
        force_kernel,
        out_shape=jax.ShapeDtypeStruct((3, atoms), F32),
        in_specs=[spec] * 3, out_specs=spec,
        scratch_shapes=[
            V((8, zlen), F32), V((8, zlen), F32), V((16, 8, rim_len), F32), V((16, 8, rim_len), F32),
            D((16,)), D((16,)), D, D],
        compiler_params=pltpu.CompilerParams(collective_id=1, has_side_effects=True, vmem_limit_bytes=32 << 20),
        name="forces",
    )(grad, rim, z)


def per_device(
    positions, attributes, edge_center, edge_other, edge_count, rim_rows, z_rows, w_emb, w_rbf, w_chan, w_lat, w_ten, w_out,
):
    rim = rim_rows[0, 0, 0]
    z = z_rows[0, 0]
    live = jnp.arange(edge_center.shape[3]) < edge_count[0, 0, 0]
    centers = jnp.where(live, edge_center[0, 0, 0], -1)
    others = jnp.where(live, edge_other[0, 0, 0], -1)
    attr_t, pos8 = table_call(attributes[0, 0, 0], positions[0, 0, 0], rim, z)
    energy, grad = edge_call(attr_t, pos8, centers, others, w_emb, w_rbf, w_chan, w_lat, w_ten, w_out)
    forces = force_call(grad, rim, z, positions.shape[4])
    return energy.reshape(1, 1, 1, -1), forces[None, None, None]


def solution(mesh):
    spread = P("gx", "gy", "gz")
    return jax.shard_map(
        per_device,
        mesh=mesh,
        in_specs=(spread,) * 7 + (P(),) * 6,
        out_specs=(spread, spread),
        check_vma=False,
    )
```

time: 1330 us -> 103 us (0.08); the launches traced: 1310 us -> 103 us
  waiting for transfers between devices: 425 us -> 0 us
  local copies, waits for them, and re-layouts: 340 us -> 5.23 us
  other arithmetic: 255 us -> 1.41 us
  starting transfers between devices: 212 us -> 0 us
  Pallas kernels: 0 us -> 94.6 us
  matrix products: 62 us -> 0 us
    ppermute x10 -> x0, waiting for transfers between devices: 425 us -> none  [the longest x4 404 us: padded(): lax.ppermute(head, axis, [((i + 1) % count, i) for i in range(count)])]
    gather x61 -> x0, local copies, waits for them, and re-layouts: 229 us -> none  [the longest x30 80.4 us: latent_of(): separation = position_table[:, others] - position_table[:, centers]]
    ppermute x10 -> x0, starting transfers between devices: 212 us -> none  [the longest x4 205 us: padded(): lax.ppermute(head, axis, [((i + 1) % count, i) for i in range(count)])]
    pallas_call x0 -> x3, Pallas kernels: none -> 94.6 us  [the longest x1 62.5 us: edge_call(): pl.pallas_call(functools.partial(edge_kernel, nb=nb, eb=eb, atoms=atoms,...]
    add_any x21 -> x0, other arithmetic: 85.6 us -> none  [the longest x6 78.6 us: latent_of(): separation = position_table[:, others] - position_table[:, centers]]
    scatter-add x11 -> x0, other arithmetic: 81.1 us -> none  [the longest x3 25.1 us: energy_terms(): gathered = tensor[centers]]
    dot_general x37 -> x0, matrix products: 62 us -> none  [the longest x15 32.6 us: latent_of(): lax.dot_general(radial, w_rbf, (((0,), (0,)), ((), ())), precision=lax.Pr...]
    while x202 -> x0, local copies, waits for them, and re-layouts: 41.6 us -> none
  transfers between devices with their start and end apart: 10 -> 0, of which waited for: 9 -> 0; matrix products, arithmetic and copies ran while one was open for 1% -> 0% of each run, Pallas kernels for 0% -> 0%
where the time goes in v1:
time: 103 us
  Pallas kernels  94.6 us (92%)
  local copies, waits for them, and re-layouts  5.23 us (5%)
  other arithmetic  1.41 us (1%)
  between operations  1.36 us (1%)
    pallas_call x1, Pallas kernels, edge_call(): pl.pallas_call(functools.partial(edge_kernel, nb=nb, eb=eb, atoms=atoms,...  62.5 us
    pallas_call x1, Pallas kernels, table_call(): pl.pallas_call(table_kernel, out_shape=(jax.ShapeDtypeStruct((adim, inner...  18.7 us
    pallas_call x1, Pallas kernels, force_call(): pl.pallas_call(force_kernel, out_shape=jax.ShapeDtypeStruct((3, atoms), F...  13.4 us
    unnamed x17, local copies, waits for them, and re-layouts  5.23 us

profile of v1, /device:TPU:1, one launch (start us, length us, event | category | flops | bytes accessed | tf_op | source)
XLA Modules:
  0.0 102.6 jit_solution(931843939544636986)
XLA Ops:
  0.6 0.0 copy-start.6
  0.6 0.0 copy-start.2
  1.3 0.7 copy.19
  2.0 0.0 copy-done.6
  2.0 1.4 %compare_select_fusion = (s32[12,1,512]{2,1,0:T(1,128)}, s32[12,1,512]{2,1,0:T(1,128)}) fusion(s32[12,1,512]{2,1,0:T(1,128)S(1)} %bitcast.20, s32[]{:T(128)} %bitcast.12, s32[12,1,512]{2,1,0:T(1,128)} %bitcast.21), kind=kLoop, calls=%fused_computation | loop fusion | flops 30720 | bytes 98308 | tf_op jit(solution)/shard_map/jit(_where)/select_n | solution.py:433
  3.4 0.0 copy-start.4
  3.4 0.0 copy-start.5
  3.4 1.5 %copy.15.w_chan_ref = bf16[256,64]{1,0:T(8,128)(2,1)} copy(bf16[256,64]{0,1:T(8,128)(2,1)} %param.22) | data formatting | bytes 65536 | tf_op args[9]
  5.0 0.0 copy-done.2
  5.0 0.0 copy-done.4
  5.0 0.0 copy-done.5
  5.0 18.7 %table.1 = (bf16[128,2688]{1,0:T(8,128)(2,1)S(1)}, f32[8,2688]{1,0:T(8,128)S(1)}) custom-call(bf16[512,128]{1,0:T(8,128)(2,1)S(1)} %bitcast.13, f32[3,512]{1,0:T(4,128)S(1)} %bitcast.14, s32[8,128]{1,0:T(8,128)S(1)} %bitcast.16, s32[1,128]{1,0:T(1,128)S(1)} %bitcast.18), custom_call_target="tpu_custom_call" | custom-call | tf_op jit(solution)/shard_map/table/pallas_call | solution.py:342
  23.7 0.0 copy-start
  23.7 0.8 copy-done
  24.6 0.0 copy-start.3
  24.6 0.6 copy-done.3
  25.2 62.5 %edges.1 = (f32[1,512]{1,0:T(1,128)}, f32[200,256]{1,0:T(8,128)}) custom-call(bf16[128,2688]{1,0:T(8,128)(2,1)} %copy-done, f32[8,2688]{1,0:T(8,128)} %copy-done.3, s32[12,1,512]{2,1,0:T(1,128)} %get-tuple-element.13.center_ref, s32[12,1,512]{2,1,0:T(1,128)} %get-tuple-element.12.other_ref, bf16[128,256]{1,0:T(8,128)(2,1)} %w_emb_ref.1, f32[8,256]{1,0:T(8,128)} %w_rbf_ref.1, ...), custom_call_target="tpu_custom_call" | custom-call | tf_op jit(solution)/shard_map/edges/pallas_call | solution.py:216
  87.6 0.0 copy-start.1
  87.6 0.9 copy-done.1
  88.6 13.4 %forces.1 = f32[3,512]{1,0:T(4,128)S(1)} custom-call(f32[200,256]{1,0:T(8,128)S(1)} %copy-done.1, s32[8,128]{1,0:T(8,128)S(1)} %bitcast.17, s32[1,128]{1,0:T(1,128)S(1)} %bitcast.19), custom_call_target="tpu_custom_call" | custom-call | tf_op jit(solution)/shard_map/forces/pallas_call | solution.py:414
  102.0 0.6 copy.16
Async XLA Ops:
  0.6 1.4 %copy-start.6 = (s32[1,1,1,6144]{3,2,1,0:T(1,128)S(1)}, s32[1,1,1,6144]{3,2,1,0:T(1,128)}, u32[]{:S(2)}) copy-start(s32[1,1,1,6144]{3,2,1,0:T(1,128)} %param.16) | copy-start | bytes 73732
  0.6 4.3 %copy-start.2 = (bf16[1,1,1,512,128]{4,3,2,1,0:T(8,128)(2,1)S(1)}, bf16[1,1,1,512,128]{4,3,2,1,0:T(8,128)(2,1)}, u32[]{:S(2)}) copy-start(bf16[1,1,1,512,128]{4,3,2,1,0:T(8,128)(2,1)} %param.14) | copy-start | bytes 393220
  3.4 1.5 %copy-start.4 = (s32[1,1,1,8,128]{4,3,2,1,0:T(8,128)S(1)}, s32[1,1,1,8,128]{4,3,2,1,0:T(8,128)}, u32[]{:S(2)}) copy-start(s32[1,1,1,8,128]{4,3,2,1,0:T(8,128)} %param.18) | copy-start | bytes 12292
  3.4 1.5 %copy-start.5 = (s32[1,1,1,128]{3,2,1,0:T(1,128)S(1)}, s32[1,1,1,128]{3,2,1,0:T(1,128)}, u32[]{:S(2)}) copy-start(s32[1,1,1,128]{3,2,1,0:T(1,128)} %param.19) | copy-start | bytes 1540
  23.7 0.9 copy-start
  24.6 0.6 copy-start.3
  87.6 0.9 copy-start.1

commit v2 on v1

v2 whole, which is shorter than its diff:
```python
import functools

import jax
import jax.numpy as jnp
from jax import lax
from jax.experimental import pallas as pl
from jax.experimental.pallas import tpu as pltpu
from jax.sharding import PartitionSpec as P

F32, BF16, I32 = jnp.float32, jnp.bfloat16, jnp.int32
ROOT3 = 3.0 ** 0.5
BANDS = (0, 1, 1, 1, 2, 2, 2, 2, 2)
BLOCK = 2048
VMEM_LIMIT = 62 << 20
MESH = pl.DeviceIdType.MESH
RIM_CELLS = [(0, 0), (0, 1), (0, 2), (1, 0), (1, 2), (2, 0), (2, 1), (2, 2)]


def source_of(position):
    if position == 0:
        return (-1, 2)
    if position == 4:
        return (1, 0)
    return (0, position - 1)


NEAR = [(0, 1), (0, -1), (1, 1), (1, -1), (-1, 1), (-1, -1), (1, 0), (-1, 0)]
CELLS = {shift: [] for shift in NEAR}
slots = 0
for row in range(5):
    for column in range(5):
        if row in (0, 4) or column in (0, 4):
            sx, ra = source_of(row)
            sy, rb = source_of(column)
            CELLS[sx, sy].append((slots, RIM_CELLS.index((ra, rb))))
            slots += 1
SLOT_ORDER = [slot for shift in NEAR for slot, _ in CELLS[shift]]


def nt(a, b):
    return lax.dot_general(a, b, (((1,), (1,)), ((), ())), preferred_element_type=F32)


def nn(a, b):
    return jnp.dot(a, b, preferred_element_type=F32)


def turned(w, unit):
    return lax.dot_general(w, unit, (((0,), (0,)), ((), ())), preferred_element_type=F32).astype(BF16)


def sigmoid(x):
    return 0.5 * jnp.tanh(0.5 * x) + 0.5


def eye(n):
    rows = lax.broadcasted_iota(I32, (n, n), 0)
    cols = lax.broadcasted_iota(I32, (n, n), 1)
    return jnp.where(rows == cols, 1.0, 0.0).astype(BF16)


def three_parts(v):
    upper = v.astype(BF16).astype(F32)
    rest = v - upper
    middle = rest.astype(BF16).astype(F32)
    return upper, middle, rest - middle


def hits(rows, index_row, offset):
    width = index_row.shape[1]
    ids = lax.broadcasted_iota(jnp.int16, (rows, width), 0)
    wanted = jnp.broadcast_to((index_row - offset).astype(jnp.int16), (rows, width))
    return jnp.where(ids == wanted, jnp.ones((), BF16), jnp.zeros((), BF16))


def whole_kernel(
    pos_ref, attr_ref, center_ref, other_ref, count_ref, rim_ref, z_ref,
    w_emb_ref, w_rbf_ref, w_chan_ref, w_lat_ref, w_ten_ref, w_out_ref,
    energy_ref, force_ref,
    tab, acc, one_c, lat_s, dsilu_s, chan_s, geo_s, dh_s, index_s, tens, tens_b, grad,
    emb_t, wrt, wchan, wcat, wback, wr2, wout_c, rim_hits,
    cells, got, inner, zcell, zgot, zlist, zback, zback_got, back_got,
    send_sem, recv_sem, zsend, zrecv, bsend, brecv, zbsend, zbrecv,
    *, block,
):
    adim, feat = w_emb_ref.shape
    ch, nbas = w_chan_ref.shape[0], w_rbf_ref.shape[0]
    atoms, edges = attr_ref.shape[0], center_ref.shape[1]
    rim_len, zlen = rim_ref.shape[1], z_ref.shape[1]
    inner_len = atoms + 16 * rim_len
    tbl = inner_len + zlen
    nb = edges // block
    nqc = atoms // 128

    i, j, k = (lax.axis_index(name) for name in ("gx", "gy", "gz"))
    nx, ny = lax.axis_size("gx"), lax.axis_size("gy")

    def at(sx, sy, side):
        return (lax.rem(i + (sx + nx), nx), lax.rem(j + (sy + ny), ny), side)

    partner = (i, j, 1 - k)
    barrier = pltpu.get_barrier_semaphore()
    for sx, sy in NEAR:
        pl.semaphore_signal(barrier, inc=1, device_id=at(sx, sy, k), device_id_type=MESH)
        pl.semaphore_signal(barrier, inc=1, device_id=at(sx, sy, 1 - k), device_id_type=MESH)
    pl.semaphore_signal(barrier, inc=1, device_id=partner, device_id_type=MESH)

    pos = jnp.concatenate([pos_ref[0], pos_ref[1], pos_ref[2]], axis=0)
    upper = pos.astype(BF16).astype(F32)
    own = jnp.concatenate(
        [nt(eye(adim), attr_ref[...]), upper, pos - upper, jnp.zeros((10, atoms), F32)], axis=0).astype(BF16)
    inner[:, 0:atoms] = own
    rim_row = jnp.concatenate([rim_ref[c:c + 1, :] for c in range(8)], axis=1)
    rim_hits[...] = hits(atoms, rim_row, 0)
    packed = nn(own, rim_hits[...]).astype(BF16)
    for n, shift in enumerate(NEAR):
        for m, (_, cell) in enumerate(CELLS[shift]):
            cells[n, m] = packed[:, cell * rim_len:(cell + 1) * rim_len]
    pl.semaphore_wait(barrier, 17)

    def rim_copy(n):
        sx, sy = NEAR[n]
        count = len(CELLS[sx, sy])
        return pltpu.make_async_remote_copy(
            src_ref=cells.at[n, 0:count], dst_ref=got.at[n, 0:count], send_sem=send_sem.at[n], recv_sem=recv_sem.at[n],
            device_id=at(-sx, -sy, k), device_id_type=MESH)

    for n in range(8):
        rim_copy(n).start()

    big_eye = eye(feat)
    emb_t[...] = turned(w_emb_ref[...], eye(adim))
    wchan[...] = turned(w_chan_ref[...], eye(ch))
    wcat[:, 0:feat] = turned(w_lat_ref[...], big_eye)
    wcat[:, feat:] = turned(w_ten_ref[...], eye(3 * ch))
    wback[0:feat, :] = w_lat_ref[...]
    wback[feat:, :] = w_ten_ref[...]
    rb = w_rbf_ref[...]
    rb_hi = rb.astype(BF16).astype(F32)
    rb_lo = rb - rb_hi
    wr2[...] = jnp.concatenate([rb_hi, rb_lo], axis=0).astype(BF16)
    wrt[...] = nt(big_eye, jnp.concatenate([rb_hi, rb_hi, rb_lo, rb_lo], axis=0).astype(BF16)).astype(BF16)
    diagonal = lax.broadcasted_iota(I32, (feat, feat), 0) == lax.broadcasted_iota(I32, (feat, feat), 1)
    wout_c[...] = jnp.sum(
        jnp.where(diagonal, jnp.broadcast_to(w_out_ref[...], (feat, feat)), 0.0), axis=1, keepdims=True)
    live = lax.broadcasted_iota(I32, (1, edges), 1) < count_ref[...]
    index_s[0:1, :] = jnp.where(live, center_ref[...], -1)
    index_s[1:2, :] = jnp.where(live, other_ref[...], -1)

    def columns(attr, place):
        emb = nn(emb_t[...], attr)
        emb = emb * sigmoid(emb)
        tail = jnp.zeros((7, place.shape[1]), F32)
        return emb.astype(BF16), jnp.concatenate(list(three_parts(place)) + [tail], axis=0)

    emb, place = columns(own[0:adim], pos)
    tab[0:feat, 0:atoms] = emb
    tab[0:feat, atoms:2 * atoms] = emb
    tab[feat:, 0:atoms] = place.astype(BF16)
    tab[feat:, atoms:2 * atoms] = (-place).astype(BF16)
    shift_cols = atoms

    def part(b):
        return pl.ds(pl.multiple_of(b * block, block), block)

    def own_part(b, _):
        c_row, o_row = index_s[0:1, part(b)], index_s[1:2, part(b)]
        a_c = hits(atoms, c_row, 0)
        one_c[:, part(b)] = a_c
        acc[:, part(b)] = nn(tab[:, 0:2 * atoms], jnp.concatenate([hits(atoms, o_row, 0), a_c], axis=0))
        return 0

    lax.fori_loop(0, nb, own_part, 0)

    moved_at = {}
    for n in range(8):
        rim_copy(n).wait_recv()
        sx, sy = NEAR[n]
        for m, (slot, _) in enumerate(CELLS[sx, sy]):
            cell = got[n, m]
            first = atoms + slot * rim_len
            tail = cell[adim:].astype(F32)
            rows = lax.broadcasted_iota(I32, (3, rim_len), 0)
            shift = jnp.where(rows == 0, float(sx), jnp.where(rows == 1, float(sy), 0.0))
            moved = tail[0:3] + tail[3:6] + shift
            moved_at[slot] = moved
            upper = moved.astype(BF16).astype(F32)
            inner[0:adim, first:first + rim_len] = cell[0:adim]
            inner[adim:, first:first + rim_len] = jnp.concatenate(
                [upper, moved - upper, jnp.zeros((10, rim_len), F32)], axis=0).astype(BF16)
    z_row = z_ref[...]
    picked = nn(inner[...], hits(inner_len, z_row, 0))
    zcell[...] = jnp.concatenate(
        [picked[0:adim + 6], (z_row >> 8).astype(F32), (z_row & 255).astype(F32), picked[adim + 8:]], axis=0).astype(BF16)
    zcopy = pltpu.make_async_remote_copy(
        src_ref=zcell, dst_ref=zgot, send_sem=zsend, recv_sem=zrecv, device_id=partner, device_id_type=MESH)
    zcopy.start()
    emb, place = columns(inner[0:adim, atoms:], jnp.concatenate([moved_at[slot] for slot in range(16)], axis=1))
    tab[0:feat, atoms + shift_cols:inner_len + shift_cols] = emb
    tab[feat:, atoms + shift_cols:inner_len + shift_cols] = place.astype(BF16)

    def cycle_part(b, _):
        o_row = index_s[1:2, part(b)]
        acc[:, part(b)] += nn(
            tab[:, atoms + shift_cols:inner_len + shift_cols], hits(inner_len - atoms, o_row, atoms))
        return 0

    lax.fori_loop(0, nb, cycle_part, 0)

    zcopy.wait_recv()
    cell = zgot[...]
    tail = cell[adim:].astype(F32)
    rows = lax.broadcasted_iota(I32, (3, zlen), 0)
    moved = tail[0:3] + tail[3:6] + jnp.where(rows == 2, (1 - 2 * k).astype(F32), 0.0)
    zlist[0:1, :] = tail[6:7] * 256.0 + tail[7:8]
    emb, place = columns(cell[0:adim], moved)
    tab[0:feat, inner_len + shift_cols:] = emb
    tab[feat:, inner_len + shift_cols:] = place.astype(BF16)

    tens[...] = jnp.zeros_like(tens)

    def geometry(sep):
        sq = jnp.sum(sep * sep, axis=0, keepdims=True)
        inv = lax.rsqrt(sq + 0.25)
        dist = (sq + 0.25) * inv
        env = 1.0 / (1.0 + sq * sq * (1.0 / 16.0))
        radii = 0.5 + 0.4 * lax.broadcasted_iota(I32, (nbas, 1), 0).astype(F32)
        t = (dist - radii) * 2.0
        gauss = jnp.exp(-(t * t))
        return sq, inv, env, t, gauss

    def phase1(b, _):
        o_row = index_s[1:2, part(b)]
        a_c = one_c[:, part(b)]
        m1 = acc[:, part(b)] + nn(tab[:, inner_len + shift_cols:], hits(zlen, o_row, inner_len))
        sep = m1[feat:feat + 3] + m1[feat + 3:feat + 6] + m1[feat + 6:feat + 9]
        sq, inv, env, t, gauss = geometry(sep)
        radial = gauss * env
        r_hi = radial.astype(BF16).astype(F32)
        r_lo = radial - r_hi
        parts = jnp.concatenate([r_hi, r_lo, r_hi, r_lo], axis=0).astype(BF16)
        mixed = m1[0:feat] + nn(wrt[...], parts)
        s = sigmoid(mixed)
        latent = (mixed * s).astype(BF16)
        lat_s[:, part(b)] = latent
        dsilu_s[:, part(b)] = (s * (1.0 + mixed * (1.0 - s))).astype(BF16)
        chan = nn(w_chan_ref[...], latent)
        chan_s[:, part(b)] = chan
        dirs = sep * inv
        x, y, z = dirs[0:1], dirs[1:2], dirs[2:3]
        harm = jnp.concatenate([
            jnp.ones_like(x), x, y, z, ROOT3 * x * y, ROOT3 * y * z, ROOT3 * z * x,
            0.5 * ROOT3 * (x * x - y * y), 0.5 * (3.0 * z * z - 1.0),
            sep, env, jnp.zeros((3, block), F32)], axis=0)
        geo_s[:, part(b)] = harm
        prod = jnp.concatenate([chan] + [chan * harm[m:m + 1] for m in range(1, 9)], axis=0).astype(BF16)
        tens[0:9 * ch] += nt(prod, a_c)
        return 0

    lax.fori_loop(0, nb, phase1, 0)
    tens_b[...] = (0.125 * tens[0:9 * ch]).astype(BF16)
    tens[...] = jnp.zeros_like(tens)

    def phase2(b, _):
        a_c = one_c[:, part(b)]
        harm = geo_s[:, part(b)]
        env = harm[12:13]
        gath = nn(tens_b[...], a_c)
        g = [gath[m * ch:(m + 1) * ch] for m in range(9)]
        h = [harm[m:m + 1] for m in range(9)]
        inv0 = g[0]
        inv1 = g[1] * h[1] + g[2] * h[2] + g[3] * h[3]
        inv2 = g[4] * h[4] + g[5] * h[5] + g[6] * h[6] + g[7] * h[7] + g[8] * h[8]
        invb = jnp.concatenate([inv0, inv1, inv2], axis=0).astype(BF16)
        pre = nn(wcat[...], jnp.concatenate([lat_s[:, part(b)], invb], axis=0))
        s = sigmoid(pre)
        wo = wout_c[...]
        e = jnp.sum(pre * s * wo, axis=0, keepdims=True)
        dpre = (s * (1.0 + pre * (1.0 - s))) * wo * env
        back = nn(wback[...], dpre.astype(BF16))
        acc[0:feat, part(b)] = back[0:feat]
        dinv = [back[feat + l * ch:feat + (l + 1) * ch] for l in range(3)]
        dh = [jnp.sum(dinv[BANDS[m]] * g[m], axis=0, keepdims=True) for m in range(1, 9)]
        en = e * env
        dh_s[:, part(b)] = jnp.concatenate([e] + dh + [jnp.zeros((7, block), F32)], axis=0)
        en_hi = en.astype(BF16).astype(F32)
        prod = jnp.concatenate(
            [dinv[0]] + [dinv[BANDS[m]] * h[m] for m in range(1, 9)] + [en_hi, en - en_hi, jnp.zeros((14, block), F32)],
            axis=0).astype(BF16)
        tens[...] += nt(prod, a_c)
        return 0

    lax.fori_loop(0, nb, phase2, 0)
    energy_ref[...] = tens[9 * ch:9 * ch + 1] + tens[9 * ch + 1:9 * ch + 2]
    tens_b[...] = (0.125 * tens[0:9 * ch]).astype(BF16)
    grad[...] = jnp.zeros_like(grad)
    q_order = list(range(nqc)) + [nqc + slot for slot in SLOT_ORDER] + [nqc + 16]
    nqo = len(q_order)

    def phase3(b, _):
        a_c = one_c[:, part(b)]
        harm = geo_s[:, part(b)]
        gd = nn(tens_b[...], a_c)
        g = [gd[m * ch:(m + 1) * ch] for m in range(9)]
        h = [harm[m:m + 1] for m in range(9)]
        chan = chan_s[:, part(b)]
        dchan = g[0]
        for m in range(1, 9):
            dchan = dchan + g[m] * h[m]
        old = dh_s[:, part(b)]
        d = [None] + [old[m:m + 1] + jnp.sum(chan * g[m], axis=0, keepdims=True) for m in range(1, 9)]
        dlat = acc[0:feat, part(b)] + nn(wchan[...], dchan.astype(BF16))
        dmixed = (dlat * dsilu_s[:, part(b)].astype(F32)).astype(BF16)
        d16 = nn(wr2[...], dmixed)
        drad = d16[0:nbas] + d16[nbas:]
        sep = harm[9:12]
        sq, inv, env, t, gauss = geometry(sep)
        dg = drad * gauss
        d_dist = jnp.sum(dg * t, axis=0, keepdims=True) * (-4.0 * env)
        d_env = jnp.sum(dg, axis=0, keepdims=True) + old[0:1]
        x, y, z = h[1], h[2], h[3]
        dx = d[1] + ROOT3 * (y * d[4] + z * d[6] + x * d[7])
        dy = d[2] + ROOT3 * (x * d[4] + z * d[5] - y * d[7])
        dz = d[3] + ROOT3 * (y * d[5] + x * d[6]) + 3.0 * z * d[8]
        d_dist = d_dist - (dx * x + dy * y + dz * z) * inv
        d_sq = d_dist * (0.5 * inv) - d_env * env * env * sq * 0.125
        dsep = jnp.concatenate([dx, dy, dz], axis=0) * inv + sep * (2.0 * d_sq)
        hi = dsep.astype(BF16).astype(F32)
        d8 = jnp.concatenate([hi, dsep - hi, jnp.zeros((2, block), F32)], axis=0)
        c_row, o_row = index_s[0:1, part(b)], index_s[1:2, part(b)]
        oq, cq = o_row >> 7, c_row >> 7
        lhs = jnp.concatenate(
            [jnp.where(oq == q, d8, 0.0) for q in q_order] + [jnp.where(cq == q, d8, 0.0) for q in range(nqc)],
            axis=0).astype(BF16)
        rhs = jnp.concatenate([hits(128, o_row & 127, 0), hits(128, c_row & 127, 0)], axis=0)
        grad[...] += nt(lhs, rhs)
        return 0

    lax.fori_loop(0, nb, phase3, 0)

    def summed(rows):
        return rows[0:3] + rows[3:6]

    first_of = {}
    rows = nqc
    for n, shift in enumerate(NEAR):
        first_of[n] = rows
        rows += len(CELLS[shift])
    zback[...] = jnp.concatenate(
        [summed(grad[(nqo - 1) * 8:nqo * 8, 0:128]), zlist[0:1, :], jnp.zeros((4, zlen), F32)], axis=0)

    def back_copy(n):
        sx, sy = NEAR[n]
        count = len(CELLS[sx, sy])
        return pltpu.make_async_remote_copy(
            src_ref=grad.at[first_of[n] * 8:(first_of[n] + count) * 8, 0:128], dst_ref=back_got.at[n, 0:count * 8],
            send_sem=bsend.at[n], recv_sem=brecv.at[n], device_id=at(sx, sy, k), device_id_type=MESH)

    def zback_copy(n):
        sx, sy = NEAR[n] if n < 8 else (0, 0)
        return pltpu.make_async_remote_copy(
            src_ref=zback, dst_ref=zback_got.at[n],
            send_sem=zbsend.at[n], recv_sem=zbrecv.at[n], device_id=at(sx, sy, 1 - k), device_id_type=MESH)

    for n in range(9):
        zback_copy(n).start()
        if n < 8:
            back_copy(n).start()

    def parts16(rows):
        return jnp.concatenate(list(three_parts(rows)) + [jnp.zeros((7, rows.shape[1]), F32)], axis=0).astype(BF16)

    def joined(rows):
        return rows[0:3] + rows[3:6] + rows[6:9]

    own_grad = jnp.concatenate(
        [summed(grad[q * 8:(q + 1) * 8, 0:128]) - summed(grad[(nqo + q) * 8:(nqo + q + 1) * 8, 128:256])
         for q in range(nqc)], axis=1)
    rim_back = [jnp.zeros((3, rim_len), F32) for _ in range(8)]
    for n in range(8, -1, -1):
        zback_copy(n).wait_recv()
        message = zback_got[n]
        values = parts16(message[0:3])
        listed = message[3:4].astype(I32)
        if n == 8:
            own_grad = own_grad + joined(nt(values, hits(atoms, listed, 0)))
        else:
            back_copy(n).wait_recv()
            for m, (slot, cell) in enumerate(CELLS[NEAR[n]]):
                from_slab = joined(nt(values, hits(rim_len, listed, atoms + slot * rim_len)))
                rim_back[cell] = rim_back[cell] + summed(back_got[n, m * 8:(m + 1) * 8]) + from_slab
    own_grad = own_grad + joined(nt(parts16(jnp.concatenate(rim_back, axis=1)), rim_hits[...]))
    for c in range(3):
        force_ref[c] = -own_grad[c:c + 1]
    for n in range(8):
        rim_copy(n).wait_send()
        back_copy(n).wait_send()
    for n in range(9):
        zback_copy(n).wait_send()
    zcopy.wait_send()


def per_device(
    positions, attributes, edge_center, edge_other, edge_count, rim_rows, z_rows, w_emb, w_rbf, w_chan, w_lat, w_ten, w_out,
):
    atoms, adim = attributes.shape[3:]
    edges, (feat, ch) = edge_center.shape[3], w_chan.shape
    rim_len, zlen = rim_rows.shape[4], z_rows.shape[3]
    inner_len = atoms + 16 * rim_len
    tbl = inner_len + zlen
    V, D = pltpu.VMEM, pltpu.SemaphoreType.DMA
    spec = pl.BlockSpec(memory_space=pltpu.VMEM)
    energy, forces = pl.pallas_call(
        functools.partial(whole_kernel, block=BLOCK),
        out_shape=(jax.ShapeDtypeStruct((1, atoms), F32), jax.ShapeDtypeStruct((3, 1, atoms), F32)),
        in_specs=[spec] * 13, out_specs=(spec, spec),
        scratch_shapes=[
            V((feat + 16, tbl + atoms), BF16), V((feat + 16, edges), F32), V((atoms, edges), BF16),
            V((feat, edges), BF16), V((feat, edges), BF16), V((ch, edges), F32), V((16, edges), F32), V((16, edges), F32),
            V((2, edges), I32), V((9 * ch + 16, atoms), F32), V((9 * ch, atoms), BF16),
            V(((tbl + atoms) // 128 * 8, 256), F32),
            V((feat, adim), BF16), V((feat, 32), BF16), V((feat, ch), BF16), V((feat, feat + 3 * ch), BF16),
            V((feat + 3 * ch, feat), BF16), V((16, feat), BF16), V((feat, 1), F32), V((atoms, 8 * rim_len), BF16),
            V((8, 3, adim + 16, rim_len), BF16), V((8, 3, adim + 16, rim_len), BF16), V((adim + 16, inner_len), BF16),
            V((adim + 16, zlen), BF16), V((adim + 16, zlen), BF16), V((8, zlen), F32), V((8, zlen), F32),
            V((9, 8, zlen), F32), V((8, 24, rim_len), F32),
            D((8,)), D((8,)), D, D, D((8,)), D((8,)), D((9,)), D((9,))],
        compiler_params=pltpu.CompilerParams(collective_id=0, has_side_effects=True, vmem_limit_bytes=VMEM_LIMIT),
        name="whole",
    )(
        positions.reshape(3, 1, atoms), attributes.reshape(atoms, adim), edge_center.reshape(1, edges),
        edge_other.reshape(1, edges), edge_count.reshape(1, 1), rim_rows.reshape(8, rim_len), z_rows.reshape(1, zlen),
        w_emb, w_rbf, w_chan.T, w_lat, w_ten, w_out.reshape(1, feat))
    return energy.reshape(1, 1, 1, atoms), forces.reshape(1, 1, 1, 3, atoms)


def solution(mesh):
    spread = P("gx", "gy", "gz")
    return jax.shard_map(
        per_device,
        mesh=mesh,
        in_specs=(spread,) * 7 + (P(),) * 6,
        out_specs=(spread, spread),
        check_vma=False,
    )
```

time: 103 us -> 69.3 us (0.67)
  Pallas kernels: 94.6 us -> 65.9 us
  local copies, waits for them, and re-layouts: 5.23 us -> 1.85 us
  other arithmetic: 1.41 us -> 0 us
    pallas_call x3 -> x1, Pallas kernels: 94.6 us -> 65.9 us  [per_device(): pl.pallas_call(functools.partial(whole_kernel, block=BLOCK), out_shape=(j...]
    unnamed x17 -> x4, local copies, waits for them, and re-layouts: 5.23 us -> 1.85 us
    select_n x1 -> x0, other arithmetic: 1.41 us -> none  [per_device(): others = jnp.where(live, edge_other[0, 0, 0], -1)]
where the time goes in v2:
time: 69.3 us; the launch traced here: 69.1 us
  Pallas kernels  65.9 us (95%)
  local copies, waits for them, and re-layouts  1.85 us (3%)
  between operations  1.3 us (2%)
    pallas_call x1, Pallas kernels, per_device(): pl.pallas_call(functools.partial(whole_kernel, block=BLOCK), out_shape=(j...  65.9 us
    unnamed x4, local copies, waits for them, and re-layouts  1.85 us

profile of v2, /device:TPU:1, one launch (start us, length us, event | category | flops | bytes accessed | tf_op | source)
XLA Modules:
  0.0 69.1 jit_solution(8595527203539352367)
XLA Ops:
  1.3 65.9 %whole.1 = (f32[1,512]{1,0:T(1,128)}, f32[3,1,512]{2,1,0:T(1,128)}) custom-call(f32[3,1,512]{2,1,0:T(1,128)} %bitcast.18, bf16[512,128]{1,0:T(8,128)(2,1)} %bitcast.14, s32[1,6144]{1,0:T(1,128)} %bitcast.16, s32[1,6144]{1,0:T(1,128)} %bitcast.17, s32[1,1]{1,0:T(1,128)} %bitcast.13.count_ref, s32[8,128]{1,0:T(8,128)} %bitcast.20, s32[1,128]{1,0:T(1,128)} %bitcast.23, ...), custom_call_target="tpu_custom_call" | custom-call | tf_op jit(solution)/shard_map/whole/pallas_call | solution.py:413
  67.2 0.0 copy-start
  67.2 1.3 %copy.19 = f32[1,1,1,512]{3,2,1,0:T(1,128)} copy(f32[1,1,1,512]{3,2,1,0:T(1,128)} %bitcast.21) | data formatting | bytes 4096
  68.5 0.0 copy-done
  68.5 0.6 copy.20
Async XLA Ops:
  67.2 1.3 %copy-start = (f32[3,1,512]{2,1,0:T(1,128)S(1)}, f32[3,1,512]{2,1,0:T(1,128)}, u32[]{:S(2)}) copy-start(f32[3,1,512]{2,1,0:T(1,128)} %get-tuple-element.5) | copy-start | bytes 18436

commit v3 on v2

--- a/solution.py
+++ b/solution.py
@@ -35,6 +35,7 @@
             CELLS[sx, sy].append((slots, RIM_CELLS.index((ra, rb))))
             slots += 1
 SLOT_ORDER = [slot for shift in NEAR for slot, _ in CELLS[shift]]
+EARLY, LATE = [(1, 3), (12, 3)], [(0, 1), (4, 8), (15, 1)]
 
 
 def nt(a, b):
@@ -73,16 +74,19 @@
     return jnp.where(ids == wanted, jnp.ones((), BF16), jnp.zeros((), BF16))
 
 
-def whole_kernel(
-    pos_ref, attr_ref, center_ref, other_ref, count_ref, rim_ref, z_ref,
-    w_emb_ref, w_rbf_ref, w_chan_ref, w_lat_ref, w_ten_ref, w_out_ref,
-    energy_ref, force_ref,
-    tab, acc, one_c, lat_s, dsilu_s, chan_s, geo_s, dh_s, index_s, tens, tens_b, grad,
-    emb_t, wrt, wchan, wcat, wback, wr2, wout_c, rim_hits,
-    cells, got, inner, zcell, zgot, zlist, zback, zback_got, back_got,
-    send_sem, recv_sem, zsend, zrecv, bsend, brecv, zbsend, zbrecv,
-    *, block,
-):
+def whole_kernel(*refs, block):
+    sources, out_ref = refs[:13], refs[13]
+    held, rest = refs[14:27], refs[27:]
+    (pos_ref, attr_ref, rim_ref, z_ref, center_ref, other_ref, count_ref,
+     w_emb_ref, w_rbf_ref, w_chan_ref, w_lat_ref, w_ten_ref, w_out_ref) = held
+    (in_sem, tab, acc, one_c, lat_s, dsilu_s, chan_s, geo_s, dh_s, index_s, tens, tens_b, grad,
+     emb_t, wrt, wchan, wcat, wback, wr2, wout_c, rim_hits, zhits,
+     cells, got, inner, zcell, zgot, zback_got, back_got,
+     send_sem, recv_sem, zsend, zrecv, bsend, brecv, zbsend, zbrecv) = rest
+
+    def fetch(n):
+        return pltpu.make_async_copy(sources[n], held[n], in_sem.at[n])
+
     adim, feat = w_emb_ref.shape
     ch, nbas = w_chan_ref.shape[0], w_rbf_ref.shape[0]
     atoms, edges = attr_ref.shape[0], center_ref.shape[1]
@@ -104,6 +108,10 @@
         pl.semaphore_signal(barrier, inc=1, device_id=at(sx, sy, k), device_id_type=MESH)
         pl.semaphore_signal(barrier, inc=1, device_id=at(sx, sy, 1 - k), device_id_type=MESH)
     pl.semaphore_signal(barrier, inc=1, device_id=partner, device_id_type=MESH)
+    for n in range(13):
+        fetch(n).start()
+    for n in range(4):
+        fetch(n).wait()
 
     pos = jnp.concatenate([pos_ref[0], pos_ref[1], pos_ref[2]], axis=0)
     upper = pos.astype(BF16).astype(F32)
@@ -111,11 +119,14 @@
         [nt(eye(adim), attr_ref[...]), upper, pos - upper, jnp.zeros((10, atoms), F32)], axis=0).astype(BF16)
     inner[:, 0:atoms] = own
     rim_row = jnp.concatenate([rim_ref[c:c + 1, :] for c in range(8)], axis=1)
-    rim_hits[...] = hits(atoms, rim_row, 0)
-    packed = nn(own, rim_hits[...]).astype(BF16)
+    rim_hits[:, 0:8 * rim_len] = hits(atoms, rim_row, 0)
+    z_row = z_ref[...]
+    z_rows = [(z_row >> 8).astype(F32), (z_row & 255).astype(F32)]
+    packed = nn(own, rim_hits[:, 0:8 * rim_len])
     for n, shift in enumerate(NEAR):
         for m, (_, cell) in enumerate(CELLS[shift]):
-            cells[n, m] = packed[:, cell * rim_len:(cell + 1) * rim_len]
+            rows = packed[:, cell * rim_len:(cell + 1) * rim_len]
+            cells[n, m] = jnp.concatenate([rows[0:adim + 6]] + z_rows + [rows[adim + 8:]], axis=0).astype(BF16)
     pl.semaphore_wait(barrier, 17)
 
     def rim_copy(n):
@@ -128,6 +139,8 @@
     for n in range(8):
         rim_copy(n).start()
 
+    for n in range(4, 13):
+        fetch(n).wait()
     big_eye = eye(feat)
     emb_t[...] = turned(w_emb_ref[...], eye(adim))
     wchan[...] = turned(w_chan_ref[...], eye(ch))
@@ -172,8 +185,11 @@
 
     lax.fori_loop(0, nb, own_part, 0)
 
+    rim_hits[:, 8 * rim_len:] = hits(atoms, z_row, 0)
     moved_at = {}
-    for n in range(8):
+    columns_of = [None] * 8
+
+    def take(n):
         rim_copy(n).wait_recv()
         sx, sy = NEAR[n]
         for m, (slot, _) in enumerate(CELLS[sx, sy]):
@@ -188,31 +204,50 @@
             inner[0:adim, first:first + rim_len] = cell[0:adim]
             inner[adim:, first:first + rim_len] = jnp.concatenate(
                 [upper, moved - upper, jnp.zeros((10, rim_len), F32)], axis=0).astype(BF16)
-    z_row = z_ref[...]
-    picked = nn(inner[...], hits(inner_len, z_row, 0))
-    zcell[...] = jnp.concatenate(
-        [picked[0:adim + 6], (z_row >> 8).astype(F32), (z_row & 255).astype(F32), picked[adim + 8:]], axis=0).astype(BF16)
+        listed = (got[n, 0][adim + 6:adim + 7].astype(F32) * 256.0 + got[n, 0][adim + 7:adim + 8].astype(F32)).astype(I32)
+        column = jnp.full_like(listed, -1)
+        for slot, cell in CELLS[-sx, -sy]:
+            row = listed - (atoms + slot * rim_len)
+            column = jnp.where((row >= 0) & (row < rim_len), row + cell * rim_len, column)
+        columns_of[NEAR.index((-sx, -sy))] = column
+
+    def fill(runs, first):
+        attr = jnp.concatenate(
+            [inner[0:adim, atoms + r * rim_len:atoms + (r + c) * rim_len] for r, c in runs], axis=1)
+        emb, place = columns(attr, jnp.concatenate([moved_at[r + q] for r, c in runs for q in range(c)], axis=1))
+        width = emb.shape[1]
+        tab[0:feat, first:first + width] = emb
+        tab[feat:, first:first + width] = place.astype(BF16)
+        return width
+
+    def add_part(runs, first, width):
+        def step(b, _):
+            o_row = index_s[1:2, part(b)]
+            picks = jnp.concatenate([hits(c * rim_len, o_row, atoms + r * rim_len) for r, c in runs], axis=0)
+            acc[:, part(b)] += nn(tab[:, first:first + width], picks)
+            return 0
+
+        lax.fori_loop(0, nb, step, 0)
+
+    for n in (6, 7):
+        take(n)
+    early = fill(EARLY, 2 * atoms)
+    add_part(EARLY, 2 * atoms, early)
+    for n in range(6):
+        take(n)
+    zcell[...] = nn(inner[...], hits(inner_len, z_row, 0)).astype(BF16)
     zcopy = pltpu.make_async_remote_copy(
         src_ref=zcell, dst_ref=zgot, send_sem=zsend, recv_sem=zrecv, device_id=partner, device_id_type=MESH)
     zcopy.start()
-    emb, place = columns(inner[0:adim, atoms:], jnp.concatenate([moved_at[slot] for slot in range(16)], axis=1))
-    tab[0:feat, atoms + shift_cols:inner_len + shift_cols] = emb
-    tab[feat:, atoms + shift_cols:inner_len + shift_cols] = place.astype(BF16)
-
-    def cycle_part(b, _):
-        o_row = index_s[1:2, part(b)]
-        acc[:, part(b)] += nn(
-            tab[:, atoms + shift_cols:inner_len + shift_cols], hits(inner_len - atoms, o_row, atoms))
-        return 0
-
-    lax.fori_loop(0, nb, cycle_part, 0)
+    late = fill(LATE, 2 * atoms + early)
+    add_part(LATE, 2 * atoms + early, late)
+    zhits[...] = hits(8 * rim_len, jnp.concatenate(columns_of, axis=1), 0)
 
     zcopy.wait_recv()
     cell = zgot[...]
     tail = cell[adim:].astype(F32)
     rows = lax.broadcasted_iota(I32, (3, zlen), 0)
     moved = tail[0:3] + tail[3:6] + jnp.where(rows == 2, (1 - 2 * k).astype(F32), 0.0)
-    zlist[0:1, :] = tail[6:7] * 256.0 + tail[7:8]
     emb, place = columns(cell[0:adim], moved)
     tab[0:feat, inner_len + shift_cols:] = emb
     tab[feat:, inner_len + shift_cols:] = place.astype(BF16)
@@ -291,7 +326,7 @@
         return 0
 
     lax.fori_loop(0, nb, phase2, 0)
-    energy_ref[...] = tens[9 * ch:9 * ch + 1] + tens[9 * ch + 1:9 * ch + 2]
+    out_ref[3] = -(tens[9 * ch:9 * ch + 1] + tens[9 * ch + 1:9 * ch + 2])
     tens_b[...] = (0.125 * tens[0:9 * ch]).astype(BF16)
     grad[...] = jnp.zeros_like(grad)
     q_order = list(range(nqc)) + [nqc + slot for slot in SLOT_ORDER] + [nqc + 16]
@@ -346,9 +381,6 @@
     for n, shift in enumerate(NEAR):
         first_of[n] = rows
         rows += len(CELLS[shift])
-    zback[...] = jnp.concatenate(
-        [summed(grad[(nqo - 1) * 8:nqo * 8, 0:128]), zlist[0:1, :], jnp.zeros((4, zlen), F32)], axis=0)
-
     def back_copy(n):
         sx, sy = NEAR[n]
         count = len(CELLS[sx, sy])
@@ -359,7 +391,7 @@
     def zback_copy(n):
         sx, sy = NEAR[n] if n < 8 else (0, 0)
         return pltpu.make_async_remote_copy(
-            src_ref=zback, dst_ref=zback_got.at[n],
+            src_ref=grad.at[(nqo - 1) * 8:nqo * 8, 0:128], dst_ref=zback_got.at[n],
             send_sem=zbsend.at[n], recv_sem=zbrecv.at[n], device_id=at(sx, sy, 1 - k), device_id_type=MESH)
 
     for n in range(9):
@@ -376,22 +408,20 @@
     own_grad = jnp.concatenate(
         [summed(grad[q * 8:(q + 1) * 8, 0:128]) - summed(grad[(nqo + q) * 8:(nqo + q + 1) * 8, 128:256])
          for q in range(nqc)], axis=1)
-    rim_back = [jnp.zeros((3, rim_len), F32) for _ in range(8)]
-    for n in range(8, -1, -1):
+    for n in range(9):
         zback_copy(n).wait_recv()
-        message = zback_got[n]
-        values = parts16(message[0:3])
-        listed = message[3:4].astype(I32)
-        if n == 8:
-            own_grad = own_grad + joined(nt(values, hits(atoms, listed, 0)))
-        else:
-            back_copy(n).wait_recv()
-            for m, (slot, cell) in enumerate(CELLS[NEAR[n]]):
-                from_slab = joined(nt(values, hits(rim_len, listed, atoms + slot * rim_len)))
-                rim_back[cell] = rim_back[cell] + summed(back_got[n, m * 8:(m + 1) * 8]) + from_slab
-    own_grad = own_grad + joined(nt(parts16(jnp.concatenate(rim_back, axis=1)), rim_hits[...]))
+    slab_back = parts16(jnp.concatenate([summed(zback_got[n]) for n in range(8)], axis=1))
+    rim_back = joined(nt(slab_back, zhits[...]))
+    added = [jnp.zeros((3, rim_len), F32) for _ in range(8)]
+    for n in range(8):
+        back_copy(n).wait_recv()
+        for m, (_, cell) in enumerate(CELLS[NEAR[n]]):
+            added[cell] = added[cell] + summed(back_got[n, m * 8:(m + 1) * 8])
+    rim_back = rim_back + jnp.concatenate(added, axis=1)
+    last = jnp.concatenate([rim_back, summed(zback_got[8])], axis=1)
+    own_grad = own_grad + joined(nt(parts16(last), rim_hits[...]))
     for c in range(3):
-        force_ref[c] = -own_grad[c:c + 1]
+        out_ref[c] = own_grad[c:c + 1]
     for n in range(8):
         rim_copy(n).wait_send()
         back_copy(n).wait_send()
@@ -409,29 +439,29 @@
     inner_len = atoms + 16 * rim_len
     tbl = inner_len + zlen
     V, D = pltpu.VMEM, pltpu.SemaphoreType.DMA
-    spec = pl.BlockSpec(memory_space=pltpu.VMEM)
-    energy, forces = pl.pallas_call(
+    arrays = (
+        positions.reshape(3, 1, atoms), attributes.reshape(atoms, adim), rim_rows.reshape(8, rim_len),
+        z_rows.reshape(1, zlen), edge_center.reshape(1, edges), edge_other.reshape(1, edges), edge_count.reshape(1, 1),
+        w_emb, w_rbf, w_chan.T, w_lat, w_ten, w_out.reshape(1, feat))
+    result = pl.pallas_call(
         functools.partial(whole_kernel, block=BLOCK),
-        out_shape=(jax.ShapeDtypeStruct((1, atoms), F32), jax.ShapeDtypeStruct((3, 1, atoms), F32)),
-        in_specs=[spec] * 13, out_specs=(spec, spec),
-        scratch_shapes=[
+        out_shape=jax.ShapeDtypeStruct((4, 1, atoms), F32),
+        in_specs=[pl.BlockSpec(memory_space=pl.ANY)] * 13, out_specs=pl.BlockSpec(memory_space=pltpu.VMEM),
+        scratch_shapes=[V(array.shape, array.dtype) for array in arrays] + [D((13,))] + [
             V((feat + 16, tbl + atoms), BF16), V((feat + 16, edges), F32), V((atoms, edges), BF16),
             V((feat, edges), BF16), V((feat, edges), BF16), V((ch, edges), F32), V((16, edges), F32), V((16, edges), F32),
             V((2, edges), I32), V((9 * ch + 16, atoms), F32), V((9 * ch, atoms), BF16),
             V(((tbl + atoms) // 128 * 8, 256), F32),
             V((feat, adim), BF16), V((feat, 32), BF16), V((feat, ch), BF16), V((feat, feat + 3 * ch), BF16),
-            V((feat + 3 * ch, feat), BF16), V((16, feat), BF16), V((feat, 1), F32), V((atoms, 8 * rim_len), BF16),
+            V((feat + 3 * ch, feat), BF16), V((16, feat), BF16), V((feat, 1), F32), V((atoms, 8 * rim_len + zlen), BF16),
+            V((8 * rim_len, 8 * zlen), BF16),
             V((8, 3, adim + 16, rim_len), BF16), V((8, 3, adim + 16, rim_len), BF16), V((adim + 16, inner_len), BF16),
-            V((adim + 16, zlen), BF16), V((adim + 16, zlen), BF16), V((8, zlen), F32), V((8, zlen), F32),
-            V((9, 8, zlen), F32), V((8, 24, rim_len), F32),
+            V((adim + 16, zlen), BF16), V((adim + 16, zlen), BF16), V((9, 8, zlen), F32), V((8, 24, rim_len), F32),
             D((8,)), D((8,)), D, D, D((8,)), D((8,)), D((9,)), D((9,))],
         compiler_params=pltpu.CompilerParams(collective_id=0, has_side_effects=True, vmem_limit_bytes=VMEM_LIMIT),
         name="whole",
-    )(
-        positions.reshape(3, 1, atoms), attributes.reshape(atoms, adim), edge_center.reshape(1, edges),
-        edge_other.reshape(1, edges), edge_count.reshape(1, 1), rim_rows.reshape(8, rim_len), z_rows.reshape(1, zlen),
-        w_emb, w_rbf, w_chan.T, w_lat, w_ten, w_out.reshape(1, feat))
-    return energy.reshape(1, 1, 1, atoms), forces.reshape(1, 1, 1, 3, atoms)
+    )(*arrays)
+    return -result[3].reshape(1, 1, 1, atoms), -result[0:3].reshape(1, 1, 1, 3, atoms)
 
 
 def solution(mesh):

time: 69.3 us -> 66.2 us (0.955)
  Pallas kernels: 65.9 us -> 62.2 us
  other arithmetic: 0 us -> 2.54 us
  local copies, waits for them, and re-layouts: 1.85 us -> 0 us
    pallas_call x1, Pallas kernels: 65.9 us -> 62.2 us  [per_device(): pl.pallas_call(functools.partial(whole_kernel, block=BLOCK), out_shape=ja...]
    unnamed x4 -> x0, local copies, waits for them, and re-layouts: 1.85 us -> none
    unnamed x0 -> x1, other arithmetic: none -> 1.29 us
    neg x0 -> x1, other arithmetic: none -> 1.25 us  [per_device(): -result[3].reshape(1, 1, 1, atoms)]
where the time goes in v3:
time: 66.2 us; the launch traced here: 66 us
  Pallas kernels  62.2 us (94%)
  other arithmetic  2.54 us (4%)
  between operations  1.29 us (2%)
    pallas_call x1, Pallas kernels, per_device(): pl.pallas_call(functools.partial(whole_kernel, block=BLOCK), out_shape=ja...  62.2 us

profile of v3, /device:TPU:1, one launch (start us, length us, event | category | flops | bytes accessed | tf_op | source)
XLA Modules:
  0.0 66.0 jit_solution(17479285248646409945)
XLA Ops:
  1.3 62.2 %whole.1 = f32[4,1,512]{2,1,0:T(1,128)} custom-call(f32[3,1,512]{2,1,0:T(1,128)} %bitcast.20, bf16[512,128]{1,0:T(8,128)(2,1)} %bitcast.16, s32[8,128]{1,0:T(8,128)} %bitcast.21, s32[1,128]{1,0:T(1,128)} %bitcast.23, s32[1,6144]{1,0:T(1,128)} %bitcast.18, s32[1,6144]{1,0:T(1,128)} %bitcast.19, s32[1,1]{1,0:T(1,128)} %bitcast.15.refs_6_, ...), custom_call_target="tpu_custom_call" | custom-call | tf_op jit(solution)/shard_map/whole/pallas_call | solution.py:446
  63.5 1.2 %negate_bitcast_fusion.1 = f32[1,1,1,512]{3,2,1,0:T(1,128)} fusion(f32[4,1,512]{2,1,0:T(1,128)} %whole.1), kind=kLoop, calls=%fused_computation.1 | loop fusion | flops 512 | bytes 4096 | tf_op jit(solution)/shard_map/neg | solution.py:464
  64.8 1.3 %negate_bitcast_fusion = f32[1,1,1,3,512]{4,2,3,1,0:T(1,128)} fusion(f32[4,1,512]{2,1,0:T(1,128)} %whole.1), kind=kLoop, calls=%fused_computation | loop fusion | flops 1536 | bytes 12288

commit v4 on v3

--- a/solution.py
+++ b/solution.py
@@ -152,7 +152,7 @@
     rb_hi = rb.astype(BF16).astype(F32)
     rb_lo = rb - rb_hi
     wr2[...] = jnp.concatenate([rb_hi, rb_lo], axis=0).astype(BF16)
-    wrt[...] = nt(big_eye, jnp.concatenate([rb_hi, rb_hi, rb_lo, rb_lo], axis=0).astype(BF16)).astype(BF16)
+    wrt[:, zlen:] = nt(big_eye, jnp.concatenate([rb_hi, rb_hi, rb_lo, rb_lo], axis=0).astype(BF16)).astype(BF16)
     diagonal = lax.broadcasted_iota(I32, (feat, feat), 0) == lax.broadcasted_iota(I32, (feat, feat), 1)
     wout_c[...] = jnp.sum(
         jnp.where(diagonal, jnp.broadcast_to(w_out_ref[...], (feat, feat)), 0.0), axis=1, keepdims=True)
@@ -249,7 +249,7 @@
     rows = lax.broadcasted_iota(I32, (3, zlen), 0)
     moved = tail[0:3] + tail[3:6] + jnp.where(rows == 2, (1 - 2 * k).astype(F32), 0.0)
     emb, place = columns(cell[0:adim], moved)
-    tab[0:feat, inner_len + shift_cols:] = emb
+    wrt[:, 0:zlen] = emb
     tab[feat:, inner_len + shift_cols:] = place.astype(BF16)
 
     tens[...] = jnp.zeros_like(tens)
@@ -267,14 +267,15 @@
     def phase1(b, _):
         o_row = index_s[1:2, part(b)]
         a_c = one_c[:, part(b)]
-        m1 = acc[:, part(b)] + nn(tab[:, inner_len + shift_cols:], hits(zlen, o_row, inner_len))
-        sep = m1[feat:feat + 3] + m1[feat + 3:feat + 6] + m1[feat + 6:feat + 9]
+        slab = hits(zlen, o_row, inner_len)
+        tail = acc[feat:, part(b)] + nn(tab[feat:, inner_len + shift_cols:], slab)
+        sep = tail[0:3] + tail[3:6] + tail[6:9]
         sq, inv, env, t, gauss = geometry(sep)
         radial = gauss * env
         r_hi = radial.astype(BF16).astype(F32)
         r_lo = radial - r_hi
         parts = jnp.concatenate([r_hi, r_lo, r_hi, r_lo], axis=0).astype(BF16)
-        mixed = m1[0:feat] + nn(wrt[...], parts)
+        mixed = acc[0:feat, part(b)] + nn(wrt[...], jnp.concatenate([slab, parts], axis=0))
         s = sigmoid(mixed)
         latent = (mixed * s).astype(BF16)
         lat_s[:, part(b)] = latent
@@ -326,7 +327,7 @@
         return 0
 
     lax.fori_loop(0, nb, phase2, 0)
-    out_ref[3] = -(tens[9 * ch:9 * ch + 1] + tens[9 * ch + 1:9 * ch + 2])
+    out_ref[3] = tens[9 * ch:9 * ch + 1] + tens[9 * ch + 1:9 * ch + 2]
     tens_b[...] = (0.125 * tens[0:9 * ch]).astype(BF16)
     grad[...] = jnp.zeros_like(grad)
     q_order = list(range(nqc)) + [nqc + slot for slot in SLOT_ORDER] + [nqc + 16]
@@ -421,13 +422,23 @@
     last = jnp.concatenate([rim_back, summed(zback_got[8])], axis=1)
     own_grad = own_grad + joined(nt(parts16(last), rim_hits[...]))
     for c in range(3):
-        out_ref[c] = own_grad[c:c + 1]
+        out_ref[c] = -own_grad[c:c + 1]
     for n in range(8):
         rim_copy(n).wait_send()
         back_copy(n).wait_send()
     for n in range(9):
         zback_copy(n).wait_send()
     zcopy.wait_send()
+
+
+def deal_kernel(result_ref, energy_ref, force_ref, sem):
+    copies = [
+        pltpu.make_async_copy(result_ref.at[3:4], energy_ref, sem.at[0]),
+        pltpu.make_async_copy(result_ref.at[0:3], force_ref, sem.at[1])]
+    for copy in copies:
+        copy.start()
+    for copy in copies:
+        copy.wait()
 
 
 def per_device(
@@ -452,7 +463,7 @@
             V((feat, edges), BF16), V((feat, edges), BF16), V((ch, edges), F32), V((16, edges), F32), V((16, edges), F32),
             V((2, edges), I32), V((9 * ch + 16, atoms), F32), V((9 * ch, atoms), BF16),
             V(((tbl + atoms) // 128 * 8, 256), F32),
-            V((feat, adim), BF16), V((feat, 32), BF16), V((feat, ch), BF16), V((feat, feat + 3 * ch), BF16),
+            V((feat, adim), BF16), V((feat, zlen + 32), BF16), V((feat, ch), BF16), V((feat, feat + 3 * ch), BF16),
             V((feat + 3 * ch, feat), BF16), V((16, feat), BF16), V((feat, 1), F32), V((atoms, 8 * rim_len + zlen), BF16),
             V((8 * rim_len, 8 * zlen), BF16),
             V((8, 3, adim + 16, rim_len), BF16), V((8, 3, adim + 16, rim_len), BF16), V((adim + 16, inner_len), BF16),
@@ -461,7 +472,13 @@
         compiler_params=pltpu.CompilerParams(collective_id=0, has_side_effects=True, vmem_limit_bytes=VMEM_LIMIT),
         name="whole",
     )(*arrays)
-    return -result[3].reshape(1, 1, 1, atoms), -result[0:3].reshape(1, 1, 1, 3, atoms)
+    anywhere = pl.BlockSpec(memory_space=pl.ANY)
+    energy, forces = pl.pallas_call(
+        deal_kernel,
+        out_shape=(jax.ShapeDtypeStruct((1, 1, atoms), F32), jax.ShapeDtypeStruct((3, 1, atoms), F32)),
+        in_specs=[anywhere], out_specs=(anywhere, anywhere), scratch_shapes=[D((2,))], name="deal",
+    )(result)
+    return energy.reshape(1, 1, 1, atoms), forces.reshape(1, 1, 1, 3, atoms)
 
 
 def solution(mesh):

time: 66.2 us -> 64.8 us (0.979)
  other arithmetic: 2.54 us -> 0 us
  Pallas kernels: 62.2 us -> 63.2 us
    pallas_call x0 -> x1, Pallas kernels: none -> 1.37 us  [per_device(): pl.pallas_call(deal_kernel, out_shape=(jax.ShapeDtypeStruct((1, 1, atoms)...]
    unnamed x1 -> x0, other arithmetic: 1.29 us -> none
    neg x1 -> x0, other arithmetic: 1.25 us -> none  [per_device(): -result[3].reshape(1, 1, 1, atoms)]
where the time goes in v4:
time: 64.8 us; the launch traced here: 64.6 us
  Pallas kernels  63.2 us (98%)
  between operations  1.45 us (2%)
    pallas_call x1, Pallas kernels, per_device(): pl.pallas_call(functools.partial(whole_kernel, block=BLOCK), out_shape=ja...  61.8 us
    pallas_call x1, Pallas kernels, per_device(): pl.pallas_call(deal_kernel, out_shape=(jax.ShapeDtypeStruct((1, 1, atoms)...  1.37 us

profile of v4, /device:TPU:1, one launch (start us, length us, event | category | flops | bytes accessed | tf_op | source)
XLA Modules:
  0.0 64.6 jit_solution(11296888744334255348)
XLA Ops:
  1.3 61.8 %whole.1.result_ref = f32[4,1,512]{2,1,0:T(1,128)} custom-call(f32[3,1,512]{2,1,0:T(1,128)} %bitcast.18, bf16[512,128]{1,0:T(8,128)(2,1)} %bitcast.14, s32[8,128]{1,0:T(8,128)} %bitcast.19, s32[1,128]{1,0:T(1,128)} %bitcast.21, s32[1,6144]{1,0:T(1,128)} %bitcast.16, s32[1,6144]{1,0:T(1,128)} %bitcast.17, s32[1,1]{1,0:T(1,128)} %bitcast.13.refs_6_, ...), custom_call_target="tpu_custom_call" | custom-call | tf_op jit(solution)/shard_map/whole/pallas_call | solution.py:457
  63.1 1.4 %deal.1 = (f32[1,1,512]{2,1,0:T(1,128)}, f32[3,1,512]{2,1,0:T(1,128)}) custom-call(f32[4,1,512]{2,1,0:T(1,128)} %whole.1.result_ref), custom_call_target="tpu_custom_call" | custom-call | tf_op jit(solution)/shard_map/deal/pallas_call | solution.py:476

commit v5 on v4

--- a/solution.py
+++ b/solution.py
@@ -10,7 +10,7 @@
 F32, BF16, I32 = jnp.float32, jnp.bfloat16, jnp.int32
 ROOT3 = 3.0 ** 0.5
 BANDS = (0, 1, 1, 1, 2, 2, 2, 2, 2)
-BLOCK = 2048
+BLOCK = 3072
 VMEM_LIMIT = 62 << 20
 MESH = pl.DeviceIdType.MESH
 RIM_CELLS = [(0, 0), (0, 1), (0, 2), (1, 0), (1, 2), (2, 0), (2, 1), (2, 2)]
@@ -35,7 +35,7 @@
             CELLS[sx, sy].append((slots, RIM_CELLS.index((ra, rb))))
             slots += 1
 SLOT_ORDER = [slot for shift in NEAR for slot, _ in CELLS[shift]]
-EARLY, LATE = [(1, 3), (12, 3)], [(0, 1), (4, 8), (15, 1)]
+EARLY, MIDDLE, LATE = [(1, 3), (12, 3)], [(5, 6)], [(0, 1), (4, 1), (11, 1), (15, 1)]
 
 
 def nt(a, b):
@@ -233,14 +233,18 @@
         take(n)
     early = fill(EARLY, 2 * atoms)
     add_part(EARLY, 2 * atoms, early)
-    for n in range(6):
+    for n in (0, 1):
+        take(n)
+    middle = fill(MIDDLE, 2 * atoms + early)
+    add_part(MIDDLE, 2 * atoms + early, middle)
+    for n in (2, 3, 4, 5):
         take(n)
     zcell[...] = nn(inner[...], hits(inner_len, z_row, 0)).astype(BF16)
     zcopy = pltpu.make_async_remote_copy(
         src_ref=zcell, dst_ref=zgot, send_sem=zsend, recv_sem=zrecv, device_id=partner, device_id_type=MESH)
     zcopy.start()
-    late = fill(LATE, 2 * atoms + early)
-    add_part(LATE, 2 * atoms + early, late)
+    late = fill(LATE, 2 * atoms + early + middle)
+    add_part(LATE, 2 * atoms + early + middle, late)
     zhits[...] = hits(8 * rim_len, jnp.concatenate(columns_of, axis=1), 0)
 
     zcopy.wait_recv()

time: 64.8 us -> 64.3 us (level)
  no operation moved by 1% of the time
where the time goes in v5:
time: 64.3 us; the launch traced here: 64.2 us
  Pallas kernels  62.7 us (98%)
  between operations  1.45 us (2%)
    pallas_call x1, Pallas kernels, per_device(): pl.pallas_call(functools.partial(whole_kernel, block=BLOCK), out_shape=ja...  61.4 us
    pallas_call x1, Pallas kernels, per_device(): pl.pallas_call(deal_kernel, out_shape=(jax.ShapeDtypeStruct((1, 1, atoms)...  1.37 us

profile of v5, /device:TPU:1, one launch (start us, length us, event | category | flops | bytes accessed | tf_op | source)
XLA Modules:
  0.0 64.2 jit_solution(4766342625245990467)
XLA Ops:
  1.3 61.4 %whole.1.result_ref = f32[4,1,512]{2,1,0:T(1,128)} custom-call(f32[3,1,512]{2,1,0:T(1,128)} %bitcast.18, bf16[512,128]{1,0:T(8,128)(2,1)} %bitcast.14, s32[8,128]{1,0:T(8,128)} %bitcast.19, s32[1,128]{1,0:T(1,128)} %bitcast.21, s32[1,6144]{1,0:T(1,128)} %bitcast.16, s32[1,6144]{1,0:T(1,128)} %bitcast.17, s32[1,1]{1,0:T(1,128)} %bitcast.13.refs_6_, ...), custom_call_target="tpu_custom_call" | custom-call | tf_op jit(solution)/shard_map/whole/pallas_call | solution.py:461
  62.6 1.4 %deal.1 = (f32[1,1,512]{2,1,0:T(1,128)}, f32[3,1,512]{2,1,0:T(1,128)}) custom-call(f32[4,1,512]{2,1,0:T(1,128)} %whole.1.result_ref), custom_call_target="tpu_custom_call" | custom-call | tf_op jit(solution)/shard_map/deal/pallas_call | solution.py:480
